TPU v7x, 32 devices: a whole 2x2x4 slice. The times are simulated.
32 devices in a mesh: dp: 8 (over z, y), tensor: 4 (over x, core).
Axes of the slice: x: 2, y: 2, z: 4, core: 2. Of those that a mesh axis runs over, the one named last changes fastest.
Arguments:
- query_act: bfloat16 [8, 1024, 1024], P('dp', None, 'tensor'), may hold values from -6 to 6
- rotated_keys: bfloat16 [8, 1024, 256], P('dp'), may hold values from -6 to 6
- value_input: bfloat16 [8, 1024, 256], P('dp'), may hold values from -6 to 6
- grad_out: bfloat16 [8, 1024, 8192], P('dp', 'tensor'), may hold values from -6 to 6
- out_weight: bfloat16 [1024, 8192], P('tensor', 'dp'), may hold values from -0.1875 to 0.1875
- doc_lengths: int32 [8, 4], P('dp'), may hold values from 1 to 512, 1024 in all within a row
Outputs:
- query_grad: bfloat16 [8, 1024, 1024], P('dp', None, 'tensor')
- key_gradient: bfloat16 [8, 4, 512, 128], P('dp', 'tensor')
- value_gradient: bfloat16 [8, 4, 512, 128], P('dp', 'tensor')
- weight_grad: float32 [1024, 8192], P('tensor', 'dp')
All inputs are finite; a program needn't handle non-finite values.
Results may differ from a plain program's by a relative error of at most 0.015.
The roundings to bfloat16 on the way count: a program that leaves them out, or rounds other values in their place, can miss the bound.
Values may be sent and summed in bfloat16 or wider, within the bound.
A program may use at most 128 MiB of HBM per device.

v0:
```python
import functools

import jax
import jax.numpy as jnp
from jax import lax
from jax.experimental import pallas as pl
from jax.experimental.pallas import tpu as pltpu
from jax.sharding import PartitionSpec as P

HEAD_SIZE = 128


MESH = pl.DeviceIdType.MESH


def ring_place(index, count):
    odd = index % 2
    return (1 - odd) * (index // 2) + odd * (count - 1 - index // 2)


def ring_index(place, count):
    back = place // (count // 2)
    return (1 - back) * (2 * place) + back * (2 * (count - 1 - place) + 1)


def exchange_kernel(
    dp_count,
    tensor_count,
    grad_ref,
    weight_ref,
    query_full,
    key_full,
    value_full,
    lengths_ref,
    query_grad_out,
    key_grad_ref,
    value_grad_ref,
    weight_grad_out,
    grads,
    weights,
    sums_out,
    sums_in,
    accum,
    query_ref,
    key_ref,
    value_ref,
    query_grad_ref,
    weight_grad_ref,
    probs,
    probs_t,
    dscores,
    outs,
    outs_t,
    kv_grads,
    kv_in,
    own_sem,
    own_weight_sem,
    near_send,
    near_recv,
    far_send,
    far_recv,
    pass_send,
    pass_recv,
    weight_send,
    weight_recv,
    sum_send,
    sum_recv,
    kv_send,
    kv_recv,
    load_sem,
    out_sem,
):
    dp_index = lax.axis_index("dp")
    tensor_index = lax.axis_index("tensor")
    chip_count = tensor_count // 2
    chip, core = tensor_index // 2, tensor_index % 2
    partner = chip * 2 + 1 - core
    place = ring_place(dp_index, dp_count)
    ring = (
        ring_index((place + 1) % dp_count, dp_count),
        ring_index((place + dp_count - 1) % dp_count, dp_count),
    )
    rows = grad_ref.shape[0]
    half = weight_ref.shape[1] // 2
    last = dp_count - 1
    seq_len, depth = query_full.shape
    heads = depth // HEAD_SIZE
    half_rows = seq_len // 2
    score_scale = HEAD_SIZE ** (-0.5)
    lead = min(2, dp_count - 2)
    kv_columns = pl.ds(pl.multiple_of(tensor_index // 2 * HEAD_SIZE, HEAD_SIZE), HEAD_SIZE)
    far_chips = [(chip + away) % chip_count for away in range(1, chip_count)]

    def place_rows(index):
        return pl.ds(pl.multiple_of(index * rows, rows), rows)

    def columns(side, step):
        if side == 0:
            owner = ring_index((place + 2 * dp_count - 1 - step) % dp_count, dp_count)
        else:
            owner = ring_index((place + 1 + step) % dp_count, dp_count)
        return pl.ds(pl.multiple_of(owner * (2 * half) + side * half, half), half)

    def own_copy(side, step):
        return pltpu.make_async_copy(
            grad_ref.at[:, columns(side, step)],
            grads.at[side, step, place_rows(tensor_index)],
            own_sem.at[side, step],
        )

    def own_weight(side):
        return pltpu.make_async_copy(
            weight_ref.at[:, pl.ds(side * half, half)],
            weights.at[side, last],
            own_weight_sem.at[side],
        )

    def near_copy(side, step):
        return pltpu.make_async_remote_copy(
            grad_ref.at[:, columns(side, step)],
            grads.at[side, step, place_rows(tensor_index)],
            near_send.at[side, step],
            near_recv.at[side, step],
            device_id=(dp_index, partner),
            device_id_type=MESH,
        )

    def far_copy(away, side, step):
        return pltpu.make_async_remote_copy(
            grad_ref.at[:, columns(side, step)],
            grads.at[side, step, place_rows(tensor_index)],
            far_send.at[away, side, step],
            far_recv.at[away, side, step],
            device_id=(dp_index, far_chips[away] * 2 + core),
            device_id_type=MESH,
        )

    def pass_copy(away, side, step):
        source = (chip + chip_count - 1 - away) % chip_count * 2 + core
        block = grads.at[side, step, place_rows(source)]
        return pltpu.make_async_remote_copy(
            block,
            block,
            pass_send.at[away, side, step],
            pass_recv.at[away, side, step],
            device_id=(dp_index, partner),
            device_id_type=MESH,
        )

    def weight_copy(side, hop):
        if isinstance(hop, int) and hop == 0:
            source = weight_ref.at[:, pl.ds(side * half, half)]
        else:
            source = weights.at[side, hop - 1]
        return pltpu.make_async_remote_copy(
            source,
            weights.at[side, hop],
            weight_send.at[side, hop],
            weight_recv.at[side, hop],
            device_id=(ring[side], tensor_index),
            device_id_type=MESH,
        )

    def sum_copy(side, step):
        return pltpu.make_async_remote_copy(
            sums_out.at[side, step],
            sums_in.at[side, step],
            sum_send.at[side, step],
            sum_recv.at[side, step],
            device_id=(ring[side], tensor_index),
            device_id_type=MESH,
        )

    loads = [
        pltpu.make_async_copy(query_full, query_ref, load_sem.at[0]),
        pltpu.make_async_copy(key_full.at[:, kv_columns], key_ref, load_sem.at[1]),
        pltpu.make_async_copy(value_full.at[:, kv_columns], value_ref, load_sem.at[2]),
    ]
    for load in loads:
        load.start()

    targets = [(dp_index, partner), (ring[0], tensor_index), (ring[1], tensor_index)]
    targets += [(dp_index, other * 2 + core) for other in far_chips]
    barrier = pltpu.get_barrier_semaphore()
    for target in targets:
        pl.semaphore_signal(barrier, inc=1, device_id=target, device_id_type=MESH)
    pl.semaphore_wait(barrier, len(targets))

    def far_start(step):
        for side in (0, 1):
            for away in range(chip_count - 1):
                far_copy(away, side, step).start()

    far_start(0)
    for side in (0, 1):
        weight_copy(side, 0).start()
        own_weight(side).start()

    @pl.loop(1, dp_count)
    def _(step):
        far_start(step)

    @pl.loop(0, dp_count)
    def _(step):
        for side in (0, 1):
            near_copy(side, step).start()
            own_copy(side, step).start()

    kv_copy = pltpu.make_async_remote_copy(
        kv_grads.at[:, pl.ds(pl.multiple_of((1 - core) * half_rows, half_rows), half_rows)],
        kv_in,
        kv_send,
        kv_recv,
        device_id=(dp_index, partner),
        device_id_type=MESH,
    )
    accum[...] = jnp.zeros_like(accum)
    kv_grads[...] = jnp.zeros_like(kv_grads)
    nt = (((1,), (1,)), ((), ()))
    tn = (((0,), (0,)), ((), ()))
    nn = (((1,), (0,)), ((), ()))
    weight_put = pltpu.make_async_copy(weight_grad_ref, weight_grad_out, out_sem.at[chip_count])

    def dot(left, right, dims):
        return lax.dot_general(left, right, dims, preferred_element_type=jnp.float32)

    def forward(block, size):
        here = pl.ds(pl.multiple_of(block * size, size), size)
        query_places = block * size + lax.broadcasted_iota(jnp.int32, (size, 1), 0)
        key_places = lax.broadcasted_iota(jnp.int32, (size, seq_len), 1)
        doc_start = jnp.zeros((size, 1), jnp.int32)
        doc_end = jnp.int32(0)
        for doc in range(lengths_ref.shape[1]):
            doc_end = doc_end + lengths_ref[0, doc]
            doc_start = jnp.where(query_places >= doc_end, doc_end, doc_start)
        allowed = (key_places >= doc_start) & (key_places <= query_places)
        keys, values = key_ref[...], value_ref[...]
        for head in range(heads):
            lanes = slice(head * HEAD_SIZE, (head + 1) * HEAD_SIZE)
            scores = dot(query_ref[here, lanes], keys, nt) * score_scale
            scores = jnp.where(allowed, scores, -jnp.inf)
            row_max = jnp.max(scores, axis=1, keepdims=True)
            total = jnp.sum(jnp.exp(scores - row_max), axis=1, keepdims=True)
            prob = jnp.exp(scores - (row_max + jnp.log(total)))
            probs[head, here] = prob
            out = jnp.dot(prob.astype(jnp.bfloat16), values, preferred_element_type=jnp.float32)
            outs[here, lanes] = out.astype(jnp.bfloat16)
            outs_t[lanes, here] = out.T.astype(jnp.bfloat16)

    def score_grads(block):
        here = place_rows(block)
        for head in range(heads):
            lanes = slice(head * HEAD_SIZE, (head + 1) * HEAD_SIZE)
            grad = accum[here, lanes].astype(jnp.bfloat16)
            delta = jnp.sum(
                grad.astype(jnp.float32) * outs[here, lanes].astype(jnp.float32), axis=1, keepdims=True
            )
            prob = probs[head, here]
            dscore = prob * (dot(grad, value_ref[...], nt) - delta) * score_scale
            dscores[head, here] = dscore.astype(jnp.bfloat16)

    def chip_rows(owner_chip):
        return pl.ds(pl.multiple_of(owner_chip * (2 * rows), 2 * rows), 2 * rows)

    def kv_part(owner_chip, part):
        here = chip_rows(owner_chip)
        to = pl.ds(pl.multiple_of(part * half_rows, half_rows), half_rows)
        key_total, value_total = kv_grads[0, to], kv_grads[1, to]
        for head in range(heads):
            lanes = slice(head * HEAD_SIZE, (head + 1) * HEAD_SIZE)
            key_total += dot(dscores[head, here, to], query_ref[here, lanes], tn)
            value_total += dot(
                probs_t[owner_chip, head, to],
                accum[here, lanes].astype(jnp.bfloat16),
                nn,
            )
        kv_grads[0, to] = key_total
        kv_grads[1, to] = value_total

    def transpose_probs(owner_chip):
        for head in range(heads):
            probs_t[owner_chip, head] = probs[head, chip_rows(owner_chip)].T.astype(jnp.bfloat16)

    def query_put(owner_chip):
        here = chip_rows(owner_chip)
        return pltpu.make_async_copy(
            query_grad_ref.at[here], query_grad_out.at[here], out_sem.at[owner_chip]
        )

    def query_part(owner_chip):
        here = chip_rows(owner_chip)
        for head in range(heads):
            lanes = slice(head * HEAD_SIZE, (head + 1) * HEAD_SIZE)
            query_grad_ref[here, lanes] = jnp.dot(
                dscores[head, here], key_ref[...], preferred_element_type=jnp.float32
            ).astype(jnp.bfloat16)
        query_put(owner_chip).start()

    def project(owner_chip, step):
        here = chip_rows(owner_chip)
        total = accum[here]
        for side in (0, 1):
            total += dot(grads[side, step, here], weights[side, step], nt)
        accum[here] = total

    def local_step(step):
        for side in (0, 1):
            own_copy(side, step).wait()
            near_copy(side, step).wait_recv()
        project(chip, step)

    def weight_step(hop, send):
        for side in (0, 1):
            weight_copy(side, hop).wait_recv()
            if send:
                weight_copy(side, hop + 1).start()

    def far_step(step):
        for side in (0, 1):
            for away in range(chip_count - 1):
                far_copy(away, side, step).wait_recv()
                pass_copy(away, side, step).start()
        for side in (0, 1):
            for away in range(chip_count - 1):
                pass_copy(away, side, step).wait_recv()

    def sum_step(step, first, final):
        for side in (0, 1):
            part = jnp.dot(
                outs_t[...], grads[side, step], preferred_element_type=jnp.float32
            )
            if not first:
                sum_copy(side, step - 1).wait_recv()
                part = part + sums_in[side, step - 1].astype(jnp.float32)
            if final:
                weight_grad_ref[:, side * half : (side + 1) * half] = part
            else:
                sums_out[side, step] = part.astype(jnp.bfloat16)
                sum_copy(side, step).start()

    def far_project(step):
        for other in far_chips:
            project(other, step)

    for load in loads:
        load.wait()
    block_rows = min(256, seq_len)
    blocks = seq_len // block_rows

    @pl.loop(0, blocks // 2)
    def _(block):
        forward(block, block_rows)

    weight_step(0, dp_count > 2)

    @pl.loop(blocks // 2, blocks)
    def _(block):
        forward(block, block_rows)

    for hop in range(1, lead):
        weight_step(hop, hop < last - 1)
    for side in (0, 1):
        own_weight(side).wait()
    local_step(last)
    for step in range(lead):
        local_step(step)

    def step_with_weights(step, first, send):
        weight_step(step + lead, send)
        local_step(step + lead)
        far_step(step)
        sum_step(step, first, False)
        far_project(step)

    step_with_weights(0, True, lead < last - 1)

    @pl.loop(1, last - 1 - lead)
    def _(step):
        step_with_weights(step, False, True)

    if last - 1 - lead > 0:
        step_with_weights(last - 1 - lead, False, False)

    @pl.loop(0, chip_count)
    def _(owner_chip):
        transpose_probs(owner_chip)

    for step in range(last - lead, last):
        far_step(step)
        sum_step(step, False, False)
        far_project(step)
        if step == last - lead:

            @pl.loop(0, 2)
            def _(block):
                score_grads(chip * 2 + block)

            kv_part(chip, 0)
            kv_part(chip, 1)
            query_part(chip)

    far_step(last)
    far_project(last)

    @pl.loop(0, tensor_count - 2)
    def _(block):
        score_grads((chip * 2 + 2 + block) % tensor_count)

    for other in far_chips:
        kv_part(other, 1 - core)
    kv_copy.start()
    sum_step(last, False, True)
    weight_put.start()
    for other in far_chips:
        query_part(other)
    for other in far_chips:
        kv_part(other, core)
    kv_copy.wait()
    mine = pl.ds(pl.multiple_of(core * half_rows, half_rows), half_rows)
    key_grad_ref[...] = (kv_grads[0, mine] + kv_in[0]).astype(jnp.bfloat16)
    value_grad_ref[...] = (kv_grads[1, mine] + kv_in[1]).astype(jnp.bfloat16)

    @pl.loop(0, dp_count)
    def _(step):
        for side in (0, 1):
            near_copy(side, step).wait_send()
            for away in range(chip_count - 1):
                far_copy(away, side, step).wait_send()
                pass_copy(away, side, step).wait_send()

    @pl.loop(1, dp_count - 1)
    def _(step):
        for side in (0, 1):
            weight_copy(side, step).wait_send()
            sum_copy(side, step).wait_send()

    weight_put.wait()

    @pl.loop(0, chip_count)
    def _(owner_chip):
        query_put(owner_chip).wait()

    for side in (0, 1):
        weight_copy(side, 0).wait_send()
        sum_copy(side, 0).wait_send()


def finish_kernel(*refs):
    count = (len(refs) - 2) // 3
    sources, results, held = refs[:count], refs[count : 2 * count], refs[2 * count : 3 * count]
    in_sem, out_sem = refs[3 * count :]
    takes = [pltpu.make_async_copy(sources[i], held[i], in_sem.at[i]) for i in range(count)]
    puts = [pltpu.make_async_copy(held[i], results[i], out_sem.at[i]) for i in range(count)]
    for take in takes:
        take.start()
    for take, put in zip(takes, puts):
        take.wait()
        put.start()
    for put in puts:
        put.wait()


def finish(*values):
    anywhere = pl.BlockSpec(memory_space=pl.ANY)
    dma = pltpu.SemaphoreType.DMA
    return pl.pallas_call(
        finish_kernel,
        out_shape=tuple(jax.ShapeDtypeStruct(value.shape, value.dtype) for value in values),
        in_specs=[anywhere] * len(values),
        out_specs=(anywhere,) * len(values),
        scratch_shapes=[pltpu.VMEM(value.shape, value.dtype) for value in values]
        + [dma((len(values),)), dma((len(values),))],
        compiler_params=pltpu.CompilerParams(vmem_limit_bytes=62 * 1024 * 1024),
        name="finish",
    )(*values)


def shards(query_act, rotated_keys, value_input, grad_out, out_weight, doc_lengths):
    dp_count, tensor_count = lax.axis_size("dp"), lax.axis_size("tensor")
    far = tensor_count // 2 - 1
    seq_len = query_act.shape[1]
    depth, width = out_weight.shape
    half = width // 2
    dma = pltpu.SemaphoreType.DMA
    vmem = pl.BlockSpec(memory_space=pltpu.VMEM)
    anywhere = pl.BlockSpec(memory_space=pl.ANY)
    kv_shape = jax.ShapeDtypeStruct((seq_len // 2, HEAD_SIZE), jnp.bfloat16)
    query_grad, key_grad, value_grad, weight_grad = pl.pallas_call(
        functools.partial(exchange_kernel, dp_count, tensor_count),
        out_shape=(
            jax.ShapeDtypeStruct((seq_len, depth), jnp.bfloat16),
            kv_shape,
            kv_shape,
            jax.ShapeDtypeStruct((depth, width), jnp.float32),
        ),
        in_specs=[
            anywhere,
            anywhere,
            anywhere,
            anywhere,
            anywhere,
            pl.BlockSpec(memory_space=pltpu.SMEM),
        ],
        out_specs=(anywhere, vmem, vmem, anywhere),
        scratch_shapes=[
            pltpu.VMEM((2, dp_count, seq_len, half), jnp.bfloat16),
            pltpu.VMEM((2, dp_count, depth, half), jnp.bfloat16),
            pltpu.VMEM((2, dp_count - 1, depth, half), jnp.bfloat16),
            pltpu.VMEM((2, dp_count - 1, depth, half), jnp.bfloat16),
            pltpu.VMEM((seq_len, depth), jnp.float32),
            pltpu.VMEM((seq_len, depth), jnp.bfloat16),
            pltpu.VMEM((seq_len, HEAD_SIZE), jnp.bfloat16),
            pltpu.VMEM((seq_len, HEAD_SIZE), jnp.bfloat16),
            pltpu.VMEM((seq_len, depth), jnp.bfloat16),
            pltpu.VMEM((depth, width), jnp.float32),
            pltpu.VMEM((depth // HEAD_SIZE, seq_len, seq_len), jnp.float32),
            pltpu.VMEM(
                (
                    tensor_count // 2,
                    depth // HEAD_SIZE,
                    seq_len,
                    seq_len // (tensor_count // 2),
                ),
                jnp.bfloat16,
            ),
            pltpu.VMEM((depth // HEAD_SIZE, seq_len, seq_len), jnp.bfloat16),
            pltpu.VMEM((seq_len, depth), jnp.bfloat16),
            pltpu.VMEM((depth, seq_len), jnp.bfloat16),
            pltpu.VMEM((2, seq_len, HEAD_SIZE), jnp.float32),
            pltpu.VMEM((2, seq_len // 2, HEAD_SIZE), jnp.float32),
            dma((2, dp_count)),
            dma((2,)),
            dma((2, dp_count)),
            dma((2, dp_count)),
            dma((far, 2, dp_count)),
            dma((far, 2, dp_count)),
            dma((far, 2, dp_count)),
            dma((far, 2, dp_count)),
            dma((2, dp_count - 1)),
            dma((2, dp_count - 1)),
            dma((2, dp_count - 1)),
            dma((2, dp_count - 1)),
            dma,
            dma,
            dma((3,)),
            dma((tensor_count // 2 + 1,)),
        ],
        compiler_params=pltpu.CompilerParams(
            collective_id=0, has_side_effects=True, vmem_limit_bytes=60 * 1024 * 1024
        ),
        name="exchange",
    )(grad_out[0], out_weight, query_act[0], rotated_keys[0], value_input[0], doc_lengths)
    query_grad, key_grad, value_grad, weight_grad = finish(
        query_grad, key_grad, value_grad, weight_grad
    )
    return (query_grad[None], key_grad[None, None], value_grad[None, None], weight_grad)


def solution(mesh):
    placed = (
        P("dp", None, "tensor"),
        P("dp", None, None),
        P("dp", None, None),
        P("dp", "tensor", None),
        P("tensor", "dp"),
        P("dp", None),
    )
    return jax.shard_map(
        shards,
        mesh=mesh,
        in_specs=placed,
        out_specs=(
            P("dp", None, "tensor"),
            P("dp", "tensor", None, None),
            P("dp", "tensor", None, None),
            P("tensor", "dp"),
        ),
        check_vma=False,
    )
```

profile of v0, /device:TPU:0, one launch (start us, length us, event | category | flops | bytes accessed | tf_op | source)
XLA Modules:
  0.0 106.8 jit_solution(17194162914088732736)
XLA Ops:
  0.6 103.5 %exchange.1 = (bf16[1024,256]{1,0:T(8,128)(2,1)}, bf16[512,128]{1,0:T(8,128)(2,1)}, bf16[512,128]{1,0:T(8,128)(2,1)}, f32[256,1024]{1,0:T(8,128)}) custom-call(bf16[256,8192]{1,0:T(8,128)(2,1)} %bitcast.7, bf16[256,1024]{1,0:T(8,128)(2,1)} %weight_ref.1, bf16[1024,256]{1,0:T(8,128)(2,1)} %bitcast.8, bf16[1024,256]{1,0:T(8,128)(2,1)} %bitcast.9, ...), custom_call_target="tpu_custom_call" | custom-call | tf_op jit(solution)/shard_map/exchange/pallas_call | solution.py:488
  104.2 2.5 %finish.1 = (bf16[1024,256]{1,0:T(8,128)(2,1)}, bf16[512,128]{1,0:T(8,128)(2,1)}, bf16[512,128]{1,0:T(8,128)(2,1)}, f32[256,1024]{1,0:T(8,128)}) custom-call(bf16[1024,256]{1,0:T(8,128)(2,1)} %get-tuple-element.12.refs_0_, bf16[512,128]{1,0:T(8,128)(2,1)} %get-tuple-element.13.refs_1_, bf16[512,128]{1,0:T(8,128)(2,1)} %get-tuple-element.14.refs_2_, ...), custom_call_target="tpu_custom_call" | custom-call | tf_op jit(solution)/shard_map/finish/pallas_call | solution.py:466
where the time goes:
time: 107 us
  Pallas kernels  106 us (99%)
    pallas_call x1, Pallas kernels, shards(): pl.pallas_call(functools.partial(exchange_kernel, dp_count, tensor_count)...  104 us
    pallas_call x1, Pallas kernels, finish(): pl.pallas_call(finish_kernel, out_shape=tuple((jax.ShapeDtypeStruct(value...  2.51 us

commit v1 on v0

v1 whole, which is shorter than its diff:
```python
import functools

import jax
import jax.numpy as jnp
from jax import lax
from jax.experimental import pallas as pl
from jax.experimental.pallas import tpu as pltpu
from jax.sharding import PartitionSpec as P

HEAD_SIZE = 128


MESH = pl.DeviceIdType.MESH


def ring_place(index, count):
    odd = index % 2
    return (1 - odd) * (index // 2) + odd * (count - 1 - index // 2)


def ring_index(place, count):
    back = place // (count // 2)
    return (1 - back) * (2 * place) + back * (2 * (count - 1 - place) + 1)


def block_sizes(seq_len, tensor_count):
    forward_rows = min(256, seq_len)
    backward_rows = min(forward_rows, 2 * seq_len // tensor_count)
    return forward_rows, backward_rows, seq_len // 2 + forward_rows


def exchange_kernel(
    dp_count,
    tensor_count,
    grad_ref,
    weight_ref,
    query_full,
    key_full,
    value_full,
    lengths_ref,
    query_grad_out,
    key_grad_ref,
    value_grad_ref,
    weight_grad_out,
    grads,
    weights,
    sums_out,
    sums_in,
    accum,
    query_ref,
    key_ref,
    value_ref,
    query_grad_ref,
    weight_grad_ref,
    probs,
    probs_t,
    outs,
    outs_t,
    share_out,
    share_in,
    back_out,
    back_in,
    kv_grads,
    kv_in,
    own_sem,
    own_weight_sem,
    near_send,
    near_recv,
    far_send,
    far_recv,
    pass_send,
    pass_recv,
    mate_send,
    mate_recv,
    weight_send,
    weight_recv,
    sum_send,
    sum_recv,
    outs_send,
    outs_recv,
    share_send,
    share_recv,
    back_send,
    back_recv,
    kv_send,
    kv_recv,
    load_sem,
    query_sem,
    put_sem,
):
    dp_index = lax.axis_index("dp")
    tensor_index = lax.axis_index("tensor")
    chip_count = tensor_count // 2
    chip, core = tensor_index // 2, tensor_index % 2
    parity = chip % 2
    mate_chip = chip + 1 - 2 * parity
    mate = mate_chip * 2 + core
    partner = chip * 2 + 1 - core
    place = ring_place(dp_index, dp_count)
    ring = (
        ring_index((place + 1) % dp_count, dp_count),
        ring_index((place + dp_count - 1) % dp_count, dp_count),
    )
    rows = grad_ref.shape[0]
    depth, width = weight_ref.shape
    half, quarter = width // 2, width // 4
    last = dp_count - 1
    seq_len = query_full.shape[0]
    heads = depth // HEAD_SIZE
    half_rows = seq_len // 2
    score_scale = HEAD_SIZE ** (-0.5)
    lead = min(3, dp_count - 2)
    forward_rows, backward_rows, window = block_sizes(seq_len, tensor_count)
    chip_blocks = 2 * rows // backward_rows
    kv_columns = pl.ds(pl.multiple_of(tensor_index // 2 * HEAD_SIZE, HEAD_SIZE), HEAD_SIZE)
    far_chips = [(chip + away) % chip_count for away in range(1, chip_count)]
    slots = (slice(0, depth), slice(depth, 2 * depth))

    def place_rows(index):
        return pl.ds(pl.multiple_of(index * rows, rows), rows)

    def own_columns(whose, side):
        return pl.ds(pl.multiple_of(whose * half + side * quarter, quarter), quarter)

    def columns(side, step, whose):
        if side == 0:
            owner = ring_index((place + 2 * dp_count - 1 - step) % dp_count, dp_count)
        else:
            owner = ring_index((place + 1 + step) % dp_count, dp_count)
        return pl.ds(
            pl.multiple_of(owner * width + whose * half + side * quarter, quarter), quarter
        )

    def remote(source, target, send, recv, dp_to, tensor_to):
        return pltpu.make_async_remote_copy(
            source, target, send, recv, device_id=(dp_to, tensor_to), device_id_type=MESH
        )

    def own_copy(side, step):
        return pltpu.make_async_copy(
            grad_ref.at[:, columns(side, step, parity)],
            grads.at[side, step, place_rows(tensor_index)],
            own_sem.at[side, step],
        )

    def own_weight(side):
        return pltpu.make_async_copy(
            weight_ref.at[:, own_columns(parity, side)],
            weights.at[side, last, slots[0]],
            own_weight_sem.at[side],
        )

    def mate_weight(side):
        return remote(
            weight_ref.at[:, own_columns(1 - parity, side)],
            weights.at[side, last, slots[1]],
            mate_send.at[side],
            mate_recv.at[side],
            dp_index,
            mate,
        )

    def near_copy(side, step):
        return remote(
            grad_ref.at[:, columns(side, step, parity)],
            grads.at[side, step, place_rows(tensor_index)],
            near_send.at[side, step],
            near_recv.at[side, step],
            dp_index,
            partner,
        )

    def far_copy(away, side, step):
        return remote(
            grad_ref.at[:, columns(side, step, far_chips[away] % 2)],
            grads.at[side, step, place_rows(tensor_index)],
            far_send.at[away, side, step],
            far_recv.at[away, side, step],
            dp_index,
            far_chips[away] * 2 + core,
        )

    def pass_copy(away, side, step):
        source = (chip + chip_count - 1 - away) % chip_count * 2 + core
        block = grads.at[side, step, place_rows(source)]
        return remote(
            block,
            block,
            pass_send.at[away, side, step],
            pass_recv.at[away, side, step],
            dp_index,
            partner,
        )

    def weight_copy(side, hop, slot):
        if isinstance(hop, int) and hop == 0:
            if slot == 0:
                source = weight_ref.at[:, own_columns(parity, side)]
            else:
                source = weights.at[side, last, slots[1]]
        else:
            source = weights.at[side, hop - 1, slots[slot]]
        return remote(
            source,
            weights.at[side, hop, slots[slot]],
            weight_send.at[side, hop, slot],
            weight_recv.at[side, hop, slot],
            ring[side],
            tensor_index,
        )

    def sum_copy(side, step, slot):
        return remote(
            sums_out.at[side, step, slots[slot]],
            sums_in.at[side, step, slots[slot]],
            sum_send.at[side, step, slot],
            sum_recv.at[side, step, slot],
            ring[side],
            tensor_index,
        )

    def block_of(owner_chip, part):
        return owner_chip * chip_blocks + part

    def block_rows(block):
        return pl.ds(pl.multiple_of(block * backward_rows, backward_rows), backward_rows)

    def share_copy(block):
        return remote(
            share_out.at[block_rows(block)],
            share_in.at[block_rows(block)],
            share_send.at[block],
            share_recv.at[block],
            dp_index,
            mate,
        )

    def back_copy(side):
        return remote(
            back_out.at[side],
            back_in.at[side],
            back_send.at[side],
            back_recv.at[side],
            dp_index,
            mate,
        )

    outs_copy = remote(outs_t.at[0], outs_t.at[1], outs_send, outs_recv, dp_index, mate)
    kv_copy = remote(
        kv_grads.at[:, pl.ds(pl.multiple_of((1 - core) * half_rows, half_rows), half_rows)],
        kv_in,
        kv_send,
        kv_recv,
        dp_index,
        partner,
    )

    loads = [
        pltpu.make_async_copy(query_full, query_ref, load_sem.at[0]),
        pltpu.make_async_copy(key_full.at[:, kv_columns], key_ref, load_sem.at[1]),
        pltpu.make_async_copy(value_full.at[:, kv_columns], value_ref, load_sem.at[2]),
    ]
    for load in loads:
        load.start()

    targets = [(dp_index, partner), (ring[0], tensor_index), (ring[1], tensor_index)]
    targets += [(dp_index, other * 2 + core) for other in far_chips]
    barrier = pltpu.get_barrier_semaphore()
    for target in targets:
        pl.semaphore_signal(barrier, inc=1, device_id=target, device_id_type=MESH)
    pl.semaphore_wait(barrier, len(targets))

    def far_start(step):
        for side in (0, 1):
            for away in range(chip_count - 1):
                far_copy(away, side, step).start()

    for side in (0, 1):
        mate_weight(side).start()
        weight_copy(side, 0, 0).start()
        own_weight(side).start()
    far_start(0)
    far_start(1)

    @pl.loop(0, dp_count)
    def _(step):
        for side in (0, 1):
            near_copy(side, step).start()
            own_copy(side, step).start()

    accum[...] = jnp.zeros_like(accum)
    kv_grads[...] = jnp.zeros_like(kv_grads)
    nt = (((1,), (1,)), ((), ()))
    tn = (((0,), (0,)), ((), ()))

    def dot(left, right, dims):
        return lax.dot_general(left, right, dims, preferred_element_type=jnp.float32)

    def window_start(index):
        skip, total = half_rows // forward_rows, seq_len // forward_rows
        past = (index + total - skip) // total
        return past * (index - skip) * forward_rows

    def window_keys(index):
        return pl.ds(pl.multiple_of(window_start(index), forward_rows), window)

    def forward(index):
        here = pl.ds(pl.multiple_of(index * forward_rows, forward_rows), forward_rows)
        query_places = index * forward_rows + lax.broadcasted_iota(jnp.int32, (forward_rows, 1), 0)
        key_places = window_start(index) + lax.broadcasted_iota(
            jnp.int32, (forward_rows, window), 1
        )
        doc_start = jnp.zeros((forward_rows, 1), jnp.int32)
        doc_end = jnp.int32(0)
        for doc in range(lengths_ref.shape[1]):
            doc_end = doc_end + lengths_ref[0, doc]
            doc_start = jnp.where(query_places >= doc_end, doc_end, doc_start)
        allowed = (key_places >= doc_start) & (key_places <= query_places)
        keys, values = key_ref[window_keys(index)], value_ref[window_keys(index)]
        for head in range(heads):
            lanes = slice(head * HEAD_SIZE, (head + 1) * HEAD_SIZE)
            scores = dot(query_ref[here, lanes], keys, nt) * score_scale
            scores = jnp.where(allowed, scores, -jnp.inf)
            row_max = jnp.max(scores, axis=1, keepdims=True)
            total = jnp.sum(jnp.exp(scores - row_max), axis=1, keepdims=True)
            prob = jnp.exp(scores - (row_max + jnp.log(total)))
            probs[head, here] = prob
            out = jnp.dot(prob.astype(jnp.bfloat16), values, preferred_element_type=jnp.float32)
            outs[here, lanes] = out.astype(jnp.bfloat16)
            outs_t[0, lanes, here] = out.T.astype(jnp.bfloat16)
            for part in range(forward_rows // backward_rows):
                piece = prob[part * backward_rows : (part + 1) * backward_rows]
                block = index * (forward_rows // backward_rows) + part
                probs_t[head, block] = piece.T.astype(jnp.bfloat16)

    def query_put(block):
        here = block_rows(block)
        return pltpu.make_async_copy(
            query_grad_ref.at[here], query_grad_out.at[here], query_sem.at[block]
        )

    def backward(block):
        here = block_rows(block)
        index = block // (forward_rows // backward_rows)
        seen = window_keys(index)
        keys, values = key_ref[seen], value_ref[seen]
        share_copy(block).wait_recv()
        key_total, value_total = kv_grads[0, seen], kv_grads[1, seen]
        for head in range(heads):
            lanes = slice(head * HEAD_SIZE, (head + 1) * HEAD_SIZE)
            grad = (accum[here, lanes] + share_in[here, lanes].astype(jnp.float32)).astype(
                jnp.bfloat16
            )
            delta = jnp.sum(
                grad.astype(jnp.float32) * outs[here, lanes].astype(jnp.float32), axis=1, keepdims=True
            )
            dscore = probs[head, here] * (dot(grad, values, nt) - delta) * score_scale
            dscore = dscore.astype(jnp.bfloat16)
            query_grad_ref[here, lanes] = jnp.dot(
                dscore, keys, preferred_element_type=jnp.float32
            ).astype(jnp.bfloat16)
            key_total += dot(dscore, query_ref[here, lanes], tn)
            value_total += jnp.dot(probs_t[head, block], grad, preferred_element_type=jnp.float32)
        kv_grads[0, seen] = key_total
        kv_grads[1, seen] = value_total
        query_put(block).start()

    def chip_rows(owner_chip):
        return pl.ds(pl.multiple_of(owner_chip * (2 * rows), 2 * rows), 2 * rows)

    def project(owner_chip, steps):
        here = chip_rows(owner_chip)
        total = accum[here]
        for step in steps:
            for side in (0, 1):
                total += dot(grads[side, step, here], weights[side, step], nt)
        accum[here] = total

    def share(owner_chip):
        for part in range(chip_blocks):
            block = block_of(owner_chip, part)
            here = block_rows(block)
            share_out[here] = accum[here, slots[1]].astype(jnp.bfloat16)
            share_copy(block).start()

    def local_wait(step):
        for side in (0, 1):
            own_copy(side, step).wait()
            near_copy(side, step).wait_recv()

    def weight_step(hop, slot, send):
        for side in (0, 1):
            weight_copy(side, hop, slot).wait_recv()
            if send:
                weight_copy(side, hop + 1, slot).start()

    def far_pass(step):
        for side in (0, 1):
            for away in range(chip_count - 1):
                far_copy(away, side, step).wait_recv()
                pass_copy(away, side, step).start()

    def pass_wait(step):
        for side in (0, 1):
            for away in range(chip_count - 1):
                pass_copy(away, side, step).wait_recv()

    def sum_part(slot, side, step):
        return jnp.dot(outs_t[slot], grads[side, step], preferred_element_type=jnp.float32)

    def sum_step(slot, step, first=False):
        for side in (0, 1):
            part = sum_part(slot, side, step)
            if not first:
                sum_copy(side, step - 1, slot).wait_recv()
                part = part + sums_in[side, step - 1, slots[slot]].astype(jnp.float32)
            sums_out[side, step, slots[slot]] = part.astype(jnp.bfloat16)
            sum_copy(side, step, slot).start()

    def sum_final(slot):
        for side in (0, 1):
            part = sum_part(slot, side, last)
            sum_copy(side, last - 1, slot).wait_recv()
            part = part + sums_in[side, last - 1, slots[slot]].astype(jnp.float32)
            if slot == 0:
                weight_grad_ref[0, :, side * quarter : (side + 1) * quarter] = part
            else:
                back_out[side] = part.astype(jnp.bfloat16)
                back_copy(side).start()

    def weight_put(which):
        whose = parity if which == 0 else 1 - parity
        to = pl.ds(pl.multiple_of(whose * half, half), half)
        return pltpu.make_async_copy(
            weight_grad_ref.at[which], weight_grad_out.at[:, to], put_sem.at[which]
        )

    for load in loads:
        load.wait()
    blocks = seq_len // forward_rows
    events = [
        lambda: weight_step(0, 0, True),
        lambda: [mate_weight(side).wait_recv() for side in (0, 1)]
        + [weight_copy(side, 0, 1).start() for side in (0, 1)],
        lambda: weight_step(1, 0, True),
    ]
    for index in range(blocks):
        forward(index)
        if index < len(events):
            events[index]()
    for event in events[blocks:]:
        event()
    outs_copy.start()

    @pl.loop(2, dp_count)
    def _(step):
        far_start(step)

    for side in (0, 1):
        own_weight(side).wait()
    weight_step(0, 1, True)
    local_wait(last)
    project(chip, [last])
    weight_step(1, 1, True)
    for step in range(2):
        local_wait(step)
    project(chip, [0, 1])
    for hop in range(2, lead):
        weight_step(hop, 0, hop < last - 1)
        weight_step(hop, 1, hop < last - 1)
        local_wait(hop)
        project(chip, [hop])
    far_pass(0)
    far_pass(1)
    outs_copy.wait_recv()
    pass_wait(0)
    sum_step(1, 0, True)

    def main_step(step, send):
        weight_step(step + lead, 0, send)
        weight_step(step + lead, 1, send)
        pass_wait(step + 1)
        sum_step(1, step + 1)
        if isinstance(step, int) and step == 0:
            sum_step(0, step, True)
        else:
            sum_step(0, step)
        local_wait(step + lead)
        project(chip, [step + lead])
        for other in far_chips:
            project(other, [step])
        far_pass(step + 2)

    steps = last - lead
    main_step(0, lead < last - 1)

    @pl.loop(1, steps - 1)
    def _(step):
        main_step(step, True)

    tail = steps - 1
    weight_step(last - 1, 0, False)
    weight_step(last - 1, 1, False)
    local_wait(last - 1)
    project(chip, [last - 1])
    share(chip)
    pass_wait(tail + 1)
    sum_step(1, tail + 1)
    sum_step(0, tail)
    for step in range(tail + 2, dp_count):
        far_pass(step)
    for other in far_chips:
        project(other, [tail, tail + 1])
    for step in range(tail + 2, dp_count):
        pass_wait(step)
    for other in far_chips:
        project(other, list(range(tail + 2, dp_count)))
        share(other)

    rest = list(range(tail + 2, last))
    order = [(mate_chip + away) % chip_count for away in range(chip_count)]
    pieces = [block_of(owner, part) for owner in order for part in range(chip_blocks)]
    per = -(-len(pieces) // max(len(rest), 1))
    for place_in, step in enumerate(rest):
        sum_step(1, step)
        sum_step(0, step - 1)
        for block in pieces[place_in * per : (place_in + 1) * per]:
            backward(block)
    for block in pieces[len(rest) * per :]:
        backward(block)
    kv_copy.start()
    sum_final(1)
    sum_step(0, last - 1)
    mine = pl.ds(pl.multiple_of(core * half_rows, half_rows), half_rows)
    kv_copy.wait()
    key_grad_ref[...] = (kv_grads[0, mine] + kv_in[0]).astype(jnp.bfloat16)
    value_grad_ref[...] = (kv_grads[1, mine] + kv_in[1]).astype(jnp.bfloat16)

    for side in (0, 1):
        mate_weight(side).wait_send()

    @pl.loop(0, dp_count)
    def _(step):
        for side in (0, 1):
            near_copy(side, step).wait_send()
            for away in range(chip_count - 1):
                far_copy(away, side, step).wait_send()
                pass_copy(away, side, step).wait_send()

    @pl.loop(0, tensor_count // 2 * chip_blocks)
    def _(block):
        share_copy(block).wait_send()
        query_put(block).wait()

    outs_copy.wait_send()
    sum_final(0)
    weight_put(0).start()
    for side in (0, 1):
        back_copy(side).wait_recv()
        weight_grad_ref[1, :, side * quarter : (side + 1) * quarter] = back_in[side].astype(
            jnp.float32
        )
    weight_put(1).start()

    for slot in (0, 1):
        for side in (0, 1):
            weight_copy(side, 0, slot).wait_send()
            sum_copy(side, 0, slot).wait_send()

    @pl.loop(1, dp_count - 1)
    def _(step):
        for slot in (0, 1):
            for side in (0, 1):
                weight_copy(side, step, slot).wait_send()
                sum_copy(side, step, slot).wait_send()

    for side in (0, 1):
        back_copy(side).wait_send()
    for which in (0, 1):
        weight_put(which).wait()


def finish_kernel(*refs):
    count = (len(refs) - 2) // 3
    sources, results, held = refs[:count], refs[count : 2 * count], refs[2 * count : 3 * count]
    in_sem, out_sem = refs[3 * count :]
    takes = [pltpu.make_async_copy(sources[i], held[i], in_sem.at[i]) for i in range(count)]
    puts = [pltpu.make_async_copy(held[i], results[i], out_sem.at[i]) for i in range(count)]
    for take in takes:
        take.start()
    for take, put in zip(takes, puts):
        take.wait()
        put.start()
    for put in puts:
        put.wait()


def finish(*values):
    anywhere = pl.BlockSpec(memory_space=pl.ANY)
    dma = pltpu.SemaphoreType.DMA
    return pl.pallas_call(
        finish_kernel,
        out_shape=tuple(jax.ShapeDtypeStruct(value.shape, value.dtype) for value in values),
        in_specs=[anywhere] * len(values),
        out_specs=(anywhere,) * len(values),
        scratch_shapes=[pltpu.VMEM(value.shape, value.dtype) for value in values]
        + [dma((len(values),)), dma((len(values),))],
        compiler_params=pltpu.CompilerParams(vmem_limit_bytes=62 * 1024 * 1024),
        name="finish",
    )(*values)


def shards(query_act, rotated_keys, value_input, grad_out, out_weight, doc_lengths):
    dp_count, tensor_count = lax.axis_size("dp"), lax.axis_size("tensor")
    chip_count = tensor_count // 2
    far = chip_count - 1
    seq_len = query_act.shape[1]
    depth, width = out_weight.shape
    half, quarter = width // 2, width // 4
    heads = depth // HEAD_SIZE
    forward_rows, backward_rows, window = block_sizes(seq_len, tensor_count)
    blocks = seq_len // backward_rows
    dma = pltpu.SemaphoreType.DMA
    vmem = pl.BlockSpec(memory_space=pltpu.VMEM)
    anywhere = pl.BlockSpec(memory_space=pl.ANY)
    kv_shape = jax.ShapeDtypeStruct((seq_len // 2, HEAD_SIZE), jnp.bfloat16)
    low, full = jnp.bfloat16, jnp.float32
    query_grad, key_grad, value_grad, weight_grad = pl.pallas_call(
        functools.partial(exchange_kernel, dp_count, tensor_count),
        out_shape=(
            jax.ShapeDtypeStruct((seq_len, depth), low),
            kv_shape,
            kv_shape,
            jax.ShapeDtypeStruct((depth, width), full),
        ),
        in_specs=[anywhere] * 5 + [pl.BlockSpec(memory_space=pltpu.SMEM)],
        out_specs=(anywhere, vmem, vmem, anywhere),
        scratch_shapes=[
            pltpu.VMEM((2, dp_count, seq_len, quarter), low),
            pltpu.VMEM((2, dp_count, 2 * depth, quarter), low),
            pltpu.VMEM((2, dp_count - 1, 2 * depth, quarter), low),
            pltpu.VMEM((2, dp_count - 1, 2 * depth, quarter), low),
            pltpu.VMEM((seq_len, 2 * depth), full),
            pltpu.VMEM((seq_len, depth), low),
            pltpu.VMEM((seq_len, HEAD_SIZE), low),
            pltpu.VMEM((seq_len, HEAD_SIZE), low),
            pltpu.VMEM((seq_len, depth), low),
            pltpu.VMEM((2, depth, half), full),
            pltpu.VMEM((heads, seq_len, window), full),
            pltpu.VMEM((heads, blocks, window, backward_rows), low),
            pltpu.VMEM((seq_len, depth), low),
            pltpu.VMEM((2, depth, seq_len), low),
            pltpu.VMEM((seq_len, depth), low),
            pltpu.VMEM((seq_len, depth), low),
            pltpu.VMEM((2, depth, quarter), low),
            pltpu.VMEM((2, depth, quarter), low),
            pltpu.VMEM((2, seq_len, HEAD_SIZE), full),
            pltpu.VMEM((2, seq_len // 2, HEAD_SIZE), full),
            dma((2, dp_count)),
            dma((2,)),
            dma((2, dp_count)),
            dma((2, dp_count)),
            dma((far, 2, dp_count)),
            dma((far, 2, dp_count)),
            dma((far, 2, dp_count)),
            dma((far, 2, dp_count)),
            dma((2,)),
            dma((2,)),
            dma((2, dp_count - 1, 2)),
            dma((2, dp_count - 1, 2)),
            dma((2, dp_count - 1, 2)),
            dma((2, dp_count - 1, 2)),
            dma,
            dma,
            dma((blocks,)),
            dma((blocks,)),
            dma((2,)),
            dma((2,)),
            dma,
            dma,
            dma((3,)),
            dma((blocks,)),
            dma((2,)),
        ],
        compiler_params=pltpu.CompilerParams(
            collective_id=0, has_side_effects=True, vmem_limit_bytes=60 * 1024 * 1024
        ),
        name="exchange",
    )(grad_out[0], out_weight, query_act[0], rotated_keys[0], value_input[0], doc_lengths)
    query_grad, key_grad, value_grad, weight_grad = finish(
        query_grad, key_grad, value_grad, weight_grad
    )
    return (query_grad[None], key_grad[None, None], value_grad[None, None], weight_grad)


def solution(mesh):
    placed = (
        P("dp", None, "tensor"),
        P("dp", None, None),
        P("dp", None, None),
        P("dp", "tensor", None),
        P("tensor", "dp"),
        P("dp", None),
    )
    return jax.shard_map(
        shards,
        mesh=mesh,
        in_specs=placed,
        out_specs=(
            P("dp", None, "tensor"),
            P("dp", "tensor", None, None),
            P("dp", "tensor", None, None),
            P("tensor", "dp"),
        ),
        check_vma=False,
    )
```

time: 107 us -> 106 us (level)
    pallas_call x1, Pallas kernels: 104 us -> 102 us  [shards(): pl.pallas_call(functools.partial(exchange_kernel, dp_count, tensor_count)...]
where the time goes in v1:
time: 106 us
  Pallas kernels  105 us (99%)
    pallas_call x1, Pallas kernels, shards(): pl.pallas_call(functools.partial(exchange_kernel, dp_count, tensor_count)...  102 us
    pallas_call x1, Pallas kernels, finish(): pl.pallas_call(finish_kernel, out_shape=tuple((jax.ShapeDtypeStruct(value...  2.51 us

profile of v1, /device:TPU:0, one launch (start us, length us, event | category | flops | bytes accessed | tf_op | source)
XLA Modules:
  0.0 105.7 jit_solution(10367919370556340488)
XLA Ops:
  0.6 102.4 %exchange.1 = (bf16[1024,256]{1,0:T(8,128)(2,1)}, bf16[512,128]{1,0:T(8,128)(2,1)}, bf16[512,128]{1,0:T(8,128)(2,1)}, f32[256,1024]{1,0:T(8,128)}) custom-call(bf16[256,8192]{1,0:T(8,128)(2,1)} %bitcast.7, bf16[256,1024]{1,0:T(8,128)(2,1)} %weight_ref.1, bf16[1024,256]{1,0:T(8,128)(2,1)} %bitcast.8, bf16[1024,256]{1,0:T(8,128)(2,1)} %bitcast.9, ...), custom_call_target="tpu_custom_call" | custom-call | tf_op jit(solution)/shard_map/exchange/pallas_call | solution.py:628
  103.1 2.5 %finish.1 = (bf16[1024,256]{1,0:T(8,128)(2,1)}, bf16[512,128]{1,0:T(8,128)(2,1)}, bf16[512,128]{1,0:T(8,128)(2,1)}, f32[256,1024]{1,0:T(8,128)}) custom-call(bf16[1024,256]{1,0:T(8,128)(2,1)} %get-tuple-element.12.refs_0_, bf16[512,128]{1,0:T(8,128)(2,1)} %get-tuple-element.13.refs_1_, bf16[512,128]{1,0:T(8,128)(2,1)} %get-tuple-element.14.refs_2_, ...), custom_call_target="tpu_custom_call" | custom-call | tf_op jit(solution)/shard_map/finish/pallas_call | solution.py:601

commit v2 on v1

--- a/solution.py
+++ b/solution.py
@@ -39,8 +39,8 @@
     value_full,
     lengths_ref,
     query_grad_out,
-    key_grad_ref,
-    value_grad_ref,
+    key_grad_out,
+    value_grad_out,
     weight_grad_out,
     grads,
     weights,
@@ -62,6 +62,7 @@
     back_in,
     kv_grads,
     kv_in,
+    kv_done,
     own_sem,
     own_weight_sem,
     near_send,
@@ -87,6 +88,7 @@
     load_sem,
     query_sem,
     put_sem,
+    kv_sem,
 ):
     dp_index = lax.axis_index("dp")
     tensor_index = lax.axis_index("tensor")
@@ -140,21 +142,21 @@
         return pltpu.make_async_copy(
             grad_ref.at[:, columns(side, step, parity)],
             grads.at[side, step, place_rows(tensor_index)],
-            own_sem.at[side, step],
+            own_sem,
         )
 
     def own_weight(side):
         return pltpu.make_async_copy(
             weight_ref.at[:, own_columns(parity, side)],
             weights.at[side, last, slots[0]],
-            own_weight_sem.at[side],
+            own_weight_sem,
         )
 
     def mate_weight(side):
         return remote(
             weight_ref.at[:, own_columns(1 - parity, side)],
             weights.at[side, last, slots[1]],
-            mate_send.at[side],
+            mate_send,
             mate_recv.at[side],
             dp_index,
             mate,
@@ -164,8 +166,8 @@
         return remote(
             grad_ref.at[:, columns(side, step, parity)],
             grads.at[side, step, place_rows(tensor_index)],
-            near_send.at[side, step],
-            near_recv.at[side, step],
+            near_send,
+            near_recv,
             dp_index,
             partner,
         )
@@ -174,8 +176,8 @@
         return remote(
             grad_ref.at[:, columns(side, step, far_chips[away] % 2)],
             grads.at[side, step, place_rows(tensor_index)],
-            far_send.at[away, side, step],
-            far_recv.at[away, side, step],
+            far_send.at[away],
+            far_recv.at[away, step],
             dp_index,
             far_chips[away] * 2 + core,
         )
@@ -186,8 +188,8 @@
         return remote(
             block,
             block,
-            pass_send.at[away, side, step],
-            pass_recv.at[away, side, step],
+            pass_send.at[away],
+            pass_recv.at[away, step],
             dp_index,
             partner,
         )
@@ -203,7 +205,7 @@
         return remote(
             source,
             weights.at[side, hop, slots[slot]],
-            weight_send.at[side, hop, slot],
+            weight_send,
             weight_recv.at[side, hop, slot],
             ring[side],
             tensor_index,
@@ -213,7 +215,7 @@
         return remote(
             sums_out.at[side, step, slots[slot]],
             sums_in.at[side, step, slots[slot]],
-            sum_send.at[side, step, slot],
+            sum_send,
             sum_recv.at[side, step, slot],
             ring[side],
             tensor_index,
@@ -229,7 +231,7 @@
         return remote(
             share_out.at[block_rows(block)],
             share_in.at[block_rows(block)],
-            share_send.at[block],
+            share_send,
             share_recv.at[block],
             dp_index,
             mate,
@@ -239,7 +241,7 @@
         return remote(
             back_out.at[side],
             back_in.at[side],
-            back_send.at[side],
+            back_send,
             back_recv.at[side],
             dp_index,
             mate,
@@ -276,11 +278,11 @@
                 far_copy(away, side, step).start()
 
     for side in (0, 1):
+        weight_copy(side, 0, 0).start()
         mate_weight(side).start()
-        weight_copy(side, 0, 0).start()
+    far_start(0)
+    for side in (0, 1):
         own_weight(side).start()
-    far_start(0)
-    far_start(1)
 
     @pl.loop(0, dp_count)
     def _(step):
@@ -336,7 +338,7 @@
     def query_put(block):
         here = block_rows(block)
         return pltpu.make_async_copy(
-            query_grad_ref.at[here], query_grad_out.at[here], query_sem.at[block]
+            query_grad_ref.at[here], query_grad_out.at[here], query_sem
         )
 
     def backward(block):
@@ -383,10 +385,13 @@
             share_out[here] = accum[here, slots[1]].astype(jnp.bfloat16)
             share_copy(block).start()
 
-    def local_wait(step):
-        for side in (0, 1):
-            own_copy(side, step).wait()
-            near_copy(side, step).wait_recv()
+    def drain(ref, sem):
+        pltpu.make_async_copy(ref, ref, sem).wait()
+
+    def local_wait():
+        drain(grads.at[:, :, place_rows(tensor_index)], own_sem)
+        drain(grads.at[:, :, place_rows(partner)], near_recv)
+        drain(weights.at[:, last, slots[0]], own_weight_sem)
 
     def weight_step(hop, slot, send):
         for side in (0, 1):
@@ -395,15 +400,16 @@
                 weight_copy(side, hop + 1, slot).start()
 
     def far_pass(step):
-        for side in (0, 1):
-            for away in range(chip_count - 1):
-                far_copy(away, side, step).wait_recv()
+        for away in range(chip_count - 1):
+            source = (chip + chip_count - 1 - away) % chip_count * 2 + core
+            drain(grads.at[:, step, place_rows(source)], far_recv.at[away, step])
+            for side in (0, 1):
                 pass_copy(away, side, step).start()
 
     def pass_wait(step):
-        for side in (0, 1):
-            for away in range(chip_count - 1):
-                pass_copy(away, side, step).wait_recv()
+        for away in range(chip_count - 1):
+            source = (chip + chip_count - 1 - away) % chip_count * 2 + 1 - core
+            drain(grads.at[:, step, place_rows(source)], pass_recv.at[away, step])
 
     def sum_part(slot, side, step):
         return jnp.dot(outs_t[slot], grads[side, step], preferred_element_type=jnp.float32)
@@ -417,100 +423,95 @@
             sums_out[side, step, slots[slot]] = part.astype(jnp.bfloat16)
             sum_copy(side, step, slot).start()
 
+    def weight_put(which, side):
+        return pltpu.make_async_copy(
+            weight_grad_ref.at[which, side],
+            weight_grad_out.at[:, own_columns(parity if which == 0 else 1 - parity, side)],
+            put_sem,
+        )
+
     def sum_final(slot):
         for side in (0, 1):
             part = sum_part(slot, side, last)
             sum_copy(side, last - 1, slot).wait_recv()
             part = part + sums_in[side, last - 1, slots[slot]].astype(jnp.float32)
             if slot == 0:
-                weight_grad_ref[0, :, side * quarter : (side + 1) * quarter] = part
+                weight_grad_ref[0, side] = part
+                weight_put(0, side).start()
             else:
                 back_out[side] = part.astype(jnp.bfloat16)
                 back_copy(side).start()
 
-    def weight_put(which):
-        whose = parity if which == 0 else 1 - parity
-        to = pl.ds(pl.multiple_of(whose * half, half), half)
-        return pltpu.make_async_copy(
-            weight_grad_ref.at[which], weight_grad_out.at[:, to], put_sem.at[which]
-        )
-
     for load in loads:
         load.wait()
     blocks = seq_len // forward_rows
-    events = [
-        lambda: weight_step(0, 0, True),
-        lambda: [mate_weight(side).wait_recv() for side in (0, 1)]
-        + [weight_copy(side, 0, 1).start() for side in (0, 1)],
-        lambda: weight_step(1, 0, True),
-    ]
-    for index in range(blocks):
+    for index in range(blocks - 1):
         forward(index)
-        if index < len(events):
-            events[index]()
-    for event in events[blocks:]:
-        event()
+    weight_step(0, 0, True)
+    forward(blocks - 1)
     outs_copy.start()
 
-    @pl.loop(2, dp_count)
+    @pl.loop(1, dp_count)
     def _(step):
         far_start(step)
 
     for side in (0, 1):
-        own_weight(side).wait()
+        mate_weight(side).wait_recv()
+        weight_copy(side, 0, 1).start()
+    local_wait()
+    project(chip, [last])
+    weight_step(1, 0, True)
     weight_step(0, 1, True)
-    local_wait(last)
-    project(chip, [last])
+    far_pass(0)
+    project(chip, [0])
+    weight_step(2, 0, True)
+    pass_wait(0)
+    sum_step(0, 0, True)
     weight_step(1, 1, True)
-    for step in range(2):
-        local_wait(step)
-    project(chip, [0, 1])
-    for hop in range(2, lead):
-        weight_step(hop, 0, hop < last - 1)
-        weight_step(hop, 1, hop < last - 1)
-        local_wait(hop)
-        project(chip, [hop])
-    far_pass(0)
+    project(chip, [1])
+    for other in far_chips:
+        project(other, [0])
+    weight_step(2, 1, True)
+    project(chip, [2])
+    outs_copy.wait_recv()
+    sum_step(1, 0, True)
+    weight_step(3, 0, True)
+    weight_step(3, 1, True)
+    project(chip, [3])
     far_pass(1)
-    outs_copy.wait_recv()
-    pass_wait(0)
-    sum_step(1, 0, True)
+    pass_wait(1)
+    sum_step(1, 1)
+    far_pass(2)
 
     def main_step(step, send):
         weight_step(step + lead, 0, send)
         weight_step(step + lead, 1, send)
         pass_wait(step + 1)
         sum_step(1, step + 1)
-        if isinstance(step, int) and step == 0:
-            sum_step(0, step, True)
-        else:
-            sum_step(0, step)
-        local_wait(step + lead)
+        sum_step(0, step)
         project(chip, [step + lead])
         for other in far_chips:
             project(other, [step])
         far_pass(step + 2)
 
-    steps = last - lead
-    main_step(0, lead < last - 1)
-
-    @pl.loop(1, steps - 1)
+    tail = last - lead - 1
+
+    @pl.loop(1, tail)
     def _(step):
         main_step(step, True)
 
-    tail = steps - 1
     weight_step(last - 1, 0, False)
     weight_step(last - 1, 1, False)
-    local_wait(last - 1)
     project(chip, [last - 1])
     share(chip)
     pass_wait(tail + 1)
     sum_step(1, tail + 1)
-    sum_step(0, tail)
-    for step in range(tail + 2, dp_count):
+    for step in range(tail + 2, last):
         far_pass(step)
     for other in far_chips:
         project(other, [tail, tail + 1])
+    sum_step(0, tail)
+    far_pass(last)
     for step in range(tail + 2, dp_count):
         pass_wait(step)
     for other in far_chips:
@@ -533,63 +534,41 @@
     sum_step(0, last - 1)
     mine = pl.ds(pl.multiple_of(core * half_rows, half_rows), half_rows)
     kv_copy.wait()
-    key_grad_ref[...] = (kv_grads[0, mine] + kv_in[0]).astype(jnp.bfloat16)
-    value_grad_ref[...] = (kv_grads[1, mine] + kv_in[1]).astype(jnp.bfloat16)
-
-    for side in (0, 1):
-        mate_weight(side).wait_send()
-
-    @pl.loop(0, dp_count)
-    def _(step):
-        for side in (0, 1):
-            near_copy(side, step).wait_send()
-            for away in range(chip_count - 1):
-                far_copy(away, side, step).wait_send()
-                pass_copy(away, side, step).wait_send()
-
-    @pl.loop(0, tensor_count // 2 * chip_blocks)
-    def _(block):
-        share_copy(block).wait_send()
-        query_put(block).wait()
-
+    kv_done[...] = (kv_grads[:, mine] + kv_in[...]).astype(jnp.bfloat16)
+    kv_puts = [
+        pltpu.make_async_copy(kv_done.at[which], to, kv_sem.at[which])
+        for which, to in enumerate((key_grad_out, value_grad_out))
+    ]
+    for put in kv_puts:
+        put.start()
+
+    drain(weights.at[:, last, slots[1]], mate_send)
+    drain(grads.at[:, :, place_rows(tensor_index)], near_send)
+    for away in range(chip_count - 1):
+        drain(grads.at[:, :, place_rows(tensor_index)], far_send.at[away])
+        drain(grads.at[:, :, place_rows(tensor_index)], pass_send.at[away])
+    drain(weights.at[:, pl.ds(0, last)], weight_send)
     outs_copy.wait_send()
+    drain(share_out, share_send)
+    drain(query_grad_ref, query_sem)
+    for put in kv_puts:
+        put.wait()
     sum_final(0)
-    weight_put(0).start()
     for side in (0, 1):
         back_copy(side).wait_recv()
-        weight_grad_ref[1, :, side * quarter : (side + 1) * quarter] = back_in[side].astype(
-            jnp.float32
-        )
-    weight_put(1).start()
-
-    for slot in (0, 1):
-        for side in (0, 1):
-            weight_copy(side, 0, slot).wait_send()
-            sum_copy(side, 0, slot).wait_send()
-
-    @pl.loop(1, dp_count - 1)
-    def _(step):
-        for slot in (0, 1):
-            for side in (0, 1):
-                weight_copy(side, step, slot).wait_send()
-                sum_copy(side, step, slot).wait_send()
-
-    for side in (0, 1):
-        back_copy(side).wait_send()
-    for which in (0, 1):
-        weight_put(which).wait()
+        weight_grad_ref[1, side] = back_in[side].astype(jnp.float32)
+        weight_put(1, side).start()
+    drain(back_out, back_send)
+    drain(sums_out, sum_send)
+    drain(weight_grad_ref, put_sem)
 
 
 def finish_kernel(*refs):
-    count = (len(refs) - 2) // 3
-    sources, results, held = refs[:count], refs[count : 2 * count], refs[2 * count : 3 * count]
-    in_sem, out_sem = refs[3 * count :]
-    takes = [pltpu.make_async_copy(sources[i], held[i], in_sem.at[i]) for i in range(count)]
-    puts = [pltpu.make_async_copy(held[i], results[i], out_sem.at[i]) for i in range(count)]
-    for take in takes:
-        take.start()
-    for take, put in zip(takes, puts):
-        take.wait()
+    count = (len(refs) - 1) // 2
+    puts = [
+        pltpu.make_async_copy(refs[i], refs[count + i], refs[2 * count].at[i]) for i in range(count)
+    ]
+    for put in puts:
         put.start()
     for put in puts:
         put.wait()
@@ -597,15 +576,13 @@
 
 def finish(*values):
     anywhere = pl.BlockSpec(memory_space=pl.ANY)
-    dma = pltpu.SemaphoreType.DMA
     return pl.pallas_call(
         finish_kernel,
-        out_shape=tuple(jax.ShapeDtypeStruct(value.shape, value.dtype) for value in values),
+        out_shape=tuple(pltpu.HBM(value.shape, value.dtype) for value in values),
         in_specs=[anywhere] * len(values),
         out_specs=(anywhere,) * len(values),
-        scratch_shapes=[pltpu.VMEM(value.shape, value.dtype) for value in values]
-        + [dma((len(values),)), dma((len(values),))],
-        compiler_params=pltpu.CompilerParams(vmem_limit_bytes=62 * 1024 * 1024),
+        scratch_shapes=[pltpu.SemaphoreType.DMA((len(values),))],
+        compiler_params=pltpu.CompilerParams(vmem_limit_bytes=8 * 1024 * 1024),
         name="finish",
     )(*values)
 
@@ -616,25 +593,25 @@
     far = chip_count - 1
     seq_len = query_act.shape[1]
     depth, width = out_weight.shape
-    half, quarter = width // 2, width // 4
+    quarter = width // 4
     heads = depth // HEAD_SIZE
     forward_rows, backward_rows, window = block_sizes(seq_len, tensor_count)
     blocks = seq_len // backward_rows
     dma = pltpu.SemaphoreType.DMA
-    vmem = pl.BlockSpec(memory_space=pltpu.VMEM)
     anywhere = pl.BlockSpec(memory_space=pl.ANY)
-    kv_shape = jax.ShapeDtypeStruct((seq_len // 2, HEAD_SIZE), jnp.bfloat16)
     low, full = jnp.bfloat16, jnp.float32
+    kv_shape = pltpu.VMEM((seq_len // 2, HEAD_SIZE), low)
     query_grad, key_grad, value_grad, weight_grad = pl.pallas_call(
         functools.partial(exchange_kernel, dp_count, tensor_count),
         out_shape=(
-            jax.ShapeDtypeStruct((seq_len, depth), low),
+            pltpu.VMEM((seq_len, depth), low),
             kv_shape,
             kv_shape,
-            jax.ShapeDtypeStruct((depth, width), full),
+            pltpu.VMEM((depth, width), full),
         ),
-        in_specs=[anywhere] * 5 + [pl.BlockSpec(memory_space=pltpu.SMEM)],
-        out_specs=(anywhere, vmem, vmem, anywhere),
+        in_specs=[pl.BlockSpec(memory_space=pltpu.HBM)] * 5
+        + [pl.BlockSpec(memory_space=pltpu.SMEM)],
+        out_specs=(anywhere,) * 4,
         scratch_shapes=[
             pltpu.VMEM((2, dp_count, seq_len, quarter), low),
             pltpu.VMEM((2, dp_count, 2 * depth, quarter), low),
@@ -645,7 +622,7 @@
             pltpu.VMEM((seq_len, HEAD_SIZE), low),
             pltpu.VMEM((seq_len, HEAD_SIZE), low),
             pltpu.VMEM((seq_len, depth), low),
-            pltpu.VMEM((2, depth, half), full),
+            pltpu.VMEM((2, 2, depth, quarter), full),
             pltpu.VMEM((heads, seq_len, window), full),
             pltpu.VMEM((heads, blocks, window, backward_rows), low),
             pltpu.VMEM((seq_len, depth), low),
@@ -656,34 +633,36 @@
             pltpu.VMEM((2, depth, quarter), low),
             pltpu.VMEM((2, seq_len, HEAD_SIZE), full),
             pltpu.VMEM((2, seq_len // 2, HEAD_SIZE), full),
-            dma((2, dp_count)),
+            pltpu.VMEM((2, seq_len // 2, HEAD_SIZE), low),
+            dma,
+            dma,
+            dma,
+            dma,
+            dma((far,)),
+            dma((far, dp_count)),
+            dma((far,)),
+            dma((far, dp_count)),
+            dma,
             dma((2,)),
-            dma((2, dp_count)),
-            dma((2, dp_count)),
-            dma((far, 2, dp_count)),
-            dma((far, 2, dp_count)),
-            dma((far, 2, dp_count)),
-            dma((far, 2, dp_count)),
+            dma,
+            dma((2, dp_count - 1, 2)),
+            dma,
+            dma((2, dp_count - 1, 2)),
+            dma,
+            dma,
+            dma,
+            dma((blocks,)),
+            dma,
             dma((2,)),
-            dma((2,)),
-            dma((2, dp_count - 1, 2)),
-            dma((2, dp_count - 1, 2)),
-            dma((2, dp_count - 1, 2)),
-            dma((2, dp_count - 1, 2)),
-            dma,
-            dma,
-            dma((blocks,)),
-            dma((blocks,)),
-            dma((2,)),
-            dma((2,)),
             dma,
             dma,
             dma((3,)),
-            dma((blocks,)),
+            dma,
+            dma,
             dma((2,)),
         ],
         compiler_params=pltpu.CompilerParams(
-            collective_id=0, has_side_effects=True, vmem_limit_bytes=60 * 1024 * 1024
+            collective_id=0, has_side_effects=True, vmem_limit_bytes=54 * 1024 * 1024
         ),
         name="exchange",
     )(grad_out[0], out_weight, query_act[0], rotated_keys[0], value_input[0], doc_lengths)

time: 106 us -> 96.4 us (0.909)
  Pallas kernels: 105 us -> 95.4 us
    pallas_call x1, Pallas kernels: 102 us -> 94.2 us  [shards(): pl.pallas_call(functools.partial(exchange_kernel, dp_count, tensor_count)...]
    pallas_call x1, Pallas kernels: 2.51 us -> 1.27 us  [finish(): pl.pallas_call(finish_kernel, out_shape=tuple((pltpu.HBM(value.shape, val...]
where the time goes in v2:
time: 96.4 us; the launch traced here: 96.2 us
  Pallas kernels  95.4 us (99%)
    pallas_call x1, Pallas kernels, shards(): pl.pallas_call(functools.partial(exchange_kernel, dp_count, tensor_count)...  94.2 us

profile of v2, /device:TPU:0, one launch (start us, length us, event | category | flops | bytes accessed | tf_op | source)
XLA Modules:
  0.0 96.2 jit_solution(16489042030580530529)
XLA Ops:
  0.6 94.2 %exchange.1 = (bf16[1024,256]{1,0:T(8,128)(2,1)S(1)}, bf16[512,128]{1,0:T(8,128)(2,1)S(1)}, bf16[512,128]{1,0:T(8,128)(2,1)S(1)}, f32[256,1024]{1,0:T(8,128)S(1)}) custom-call(bf16[256,8192]{1,0:T(8,128)(2,1)} %bitcast.7, bf16[256,1024]{1,0:T(8,128)(2,1)} %weight_ref.1, bf16[1024,256]{1,0:T(8,128)(2,1)} %bitcast.8, bf16[1024,256]{1,0:T(8,128)(2,1)} %bitcast.9, ...), custom_call_target="tpu_custom_call" | custom-call | tf_op jit(solution)/shard_map/exchange/pallas_call | solution.py:604
  94.8 1.3 %finish.1 = (bf16[1024,256]{1,0:T(8,128)(2,1)}, bf16[512,128]{1,0:T(8,128)(2,1)}, bf16[512,128]{1,0:T(8,128)(2,1)}, f32[256,1024]{1,0:T(8,128)}) custom-call(bf16[1024,256]{1,0:T(8,128)(2,1)S(1)} %get-tuple-element.12.refs_0_, bf16[512,128]{1,0:T(8,128)(2,1)S(1)} %get-tuple-element.13.refs_1_, bf16[512,128]{1,0:T(8,128)(2,1)S(1)} %get-tuple-element.14.refs_2_, ...), custom_call_target="tpu_custom_call" | custom-call | tf_op jit(solution)/shard_map/finish/pallas_call | solution.py:579

commit v3 on v2

--- a/solution.py
+++ b/solution.py
@@ -111,7 +111,7 @@
     heads = depth // HEAD_SIZE
     half_rows = seq_len // 2
     score_scale = HEAD_SIZE ** (-0.5)
-    lead = min(3, dp_count - 2)
+    middle = dp_count // 2
     forward_rows, backward_rows, window = block_sizes(seq_len, tensor_count)
     chip_blocks = 2 * rows // backward_rows
     kv_columns = pl.ds(pl.multiple_of(tensor_index // 2 * HEAD_SIZE, HEAD_SIZE), HEAD_SIZE)
@@ -194,20 +194,23 @@
             partner,
         )
 
-    def weight_copy(side, hop, slot):
-        if isinstance(hop, int) and hop == 0:
-            if slot == 0:
-                source = weight_ref.at[:, own_columns(parity, side)]
-            else:
-                source = weights.at[side, last, slots[1]]
+    def hop_step(hop, minor):
+        return last - hop if minor else hop - 1
+
+    def weight_copy(side, hop, minor, slot):
+        if hop > 1:
+            source = weights.at[side, hop_step(hop - 1, minor), slots[slot]]
+        elif slot == 0:
+            source = weight_ref.at[:, own_columns(parity, side)]
         else:
-            source = weights.at[side, hop - 1, slots[slot]]
+            source = weights.at[side, last, slots[1]]
+        step = hop_step(hop, minor)
         return remote(
             source,
-            weights.at[side, hop, slots[slot]],
+            weights.at[side, step, slots[slot]],
             weight_send,
-            weight_recv.at[side, hop, slot],
-            ring[side],
+            weight_recv.at[side, step, slot],
+            ring[1 - side if minor else side],
             tensor_index,
         )
 
@@ -217,7 +220,7 @@
             sums_in.at[side, step, slots[slot]],
             sum_send,
             sum_recv.at[side, step, slot],
-            ring[side],
+            ring[side if step >= middle - 1 else 1 - side],
             tensor_index,
         )
 
@@ -277,10 +280,16 @@
             for away in range(chip_count - 1):
                 far_copy(away, side, step).start()
 
+    grad_order = []
+    for turn in range(middle):
+        grad_order += [middle - 1 + turn] + ([middle - 2 - turn] if turn < middle - 1 else [])
+    grad_order.append(last)
     for side in (0, 1):
-        weight_copy(side, 0, 0).start()
+        weight_copy(side, 1, 0, 0).start()
         mate_weight(side).start()
-    far_start(0)
+    for side in (0, 1):
+        weight_copy(side, 1, 1, 0).start()
+    far_start(grad_order[0])
     for side in (0, 1):
         own_weight(side).start()
 
@@ -290,8 +299,6 @@
             near_copy(side, step).start()
             own_copy(side, step).start()
 
-    accum[...] = jnp.zeros_like(accum)
-    kv_grads[...] = jnp.zeros_like(kv_grads)
     nt = (((1,), (1,)), ((), ()))
     tn = (((0,), (0,)), ((), ()))
 
@@ -393,11 +400,11 @@
         drain(grads.at[:, :, place_rows(partner)], near_recv)
         drain(weights.at[:, last, slots[0]], own_weight_sem)
 
-    def weight_step(hop, slot, send):
+    def weight_step(hop, minor, slot):
         for side in (0, 1):
-            weight_copy(side, hop, slot).wait_recv()
-            if send:
-                weight_copy(side, hop + 1, slot).start()
+            weight_copy(side, hop, minor, slot).wait_recv()
+            if hop + minor < middle:
+                weight_copy(side, hop + 1, minor, slot).start()
 
     def far_pass(step):
         for away in range(chip_count - 1):
@@ -411,15 +418,25 @@
             source = (chip + chip_count - 1 - away) % chip_count * 2 + 1 - core
             drain(grads.at[:, step, place_rows(source)], pass_recv.at[away, step])
 
+    passed = set()
+
+    def pass_wait_once(step):
+        if step not in passed:
+            passed.add(step)
+            pass_wait(step)
+
     def sum_part(slot, side, step):
         return jnp.dot(outs_t[slot], grads[side, step], preferred_element_type=jnp.float32)
 
-    def sum_step(slot, step, first=False):
+    def sum_step(slot, step):
+        pass_wait_once(step)
+        before = step - 1 if step >= middle - 1 else step + 1
+        first = step in (middle - 2, middle - 1)
         for side in (0, 1):
             part = sum_part(slot, side, step)
             if not first:
-                sum_copy(side, step - 1, slot).wait_recv()
-                part = part + sums_in[side, step - 1, slots[slot]].astype(jnp.float32)
+                sum_copy(side, before, slot).wait_recv()
+                part = part + sums_in[side, before, slots[slot]].astype(jnp.float32)
             sums_out[side, step, slots[slot]] = part.astype(jnp.bfloat16)
             sum_copy(side, step, slot).start()
 
@@ -433,8 +450,9 @@
     def sum_final(slot):
         for side in (0, 1):
             part = sum_part(slot, side, last)
-            sum_copy(side, last - 1, slot).wait_recv()
-            part = part + sums_in[side, last - 1, slots[slot]].astype(jnp.float32)
+            for before in (0, last - 1):
+                sum_copy(side, before, slot).wait_recv()
+                part = part + sums_in[side, before, slots[slot]].astype(jnp.float32)
             if slot == 0:
                 weight_grad_ref[0, side] = part
                 weight_put(0, side).start()
@@ -447,91 +465,83 @@
     blocks = seq_len // forward_rows
     for index in range(blocks - 1):
         forward(index)
-    weight_step(0, 0, True)
+    weight_step(1, 0, 0)
     forward(blocks - 1)
     outs_copy.start()
-
-    @pl.loop(1, dp_count)
-    def _(step):
+    for step in grad_order[1:]:
         far_start(step)
-
     for side in (0, 1):
         mate_weight(side).wait_recv()
-        weight_copy(side, 0, 1).start()
+        for minor in (0, 1):
+            weight_copy(side, 1, minor, 1).start()
+    weight_step(1, 1, 0)
+    accum[...] = jnp.zeros_like(accum)
+    kv_grads[...] = jnp.zeros_like(kv_grads)
     local_wait()
     project(chip, [last])
-    weight_step(1, 0, True)
-    weight_step(0, 1, True)
-    far_pass(0)
-    project(chip, [0])
-    weight_step(2, 0, True)
-    pass_wait(0)
-    sum_step(0, 0, True)
-    weight_step(1, 1, True)
-    project(chip, [1])
+    passing = list(grad_order)
+
+    def pass_next():
+        far_pass(passing.pop(0))
+
+    for hop in range(2, middle + 1):
+        weight_step(hop, 0, 0)
+        weight_step(hop - 1, 0, 1)
+        weight_step(hop - 1, 1, 1)
+        if hop < middle:
+            weight_step(hop, 1, 0)
+        if hop == middle - 2:
+            pass_next()
+        project(chip, [hop - 2, last + 1 - hop])
+        if hop == middle - 2:
+            sum_step(0, middle - 1)
+        if hop == middle - 1:
+            outs_copy.wait_recv()
+            sum_step(1, middle - 1)
+            pass_next()
+    sum_step(0, middle - 2)
+    weight_step(middle, 0, 1)
+    sum_step(1, middle - 2)
+    pass_next()
+    pass_next()
+    project(chip, [middle - 1])
+    share(chip)
     for other in far_chips:
-        project(other, [0])
-    weight_step(2, 1, True)
-    project(chip, [2])
-    outs_copy.wait_recv()
-    sum_step(1, 0, True)
-    weight_step(3, 0, True)
-    weight_step(3, 1, True)
-    project(chip, [3])
-    far_pass(1)
-    pass_wait(1)
-    sum_step(1, 1)
-    far_pass(2)
-
-    def main_step(step, send):
-        weight_step(step + lead, 0, send)
-        weight_step(step + lead, 1, send)
-        pass_wait(step + 1)
-        sum_step(1, step + 1)
-        sum_step(0, step)
-        project(chip, [step + lead])
-        for other in far_chips:
-            project(other, [step])
-        far_pass(step + 2)
-
-    tail = last - lead - 1
-
-    @pl.loop(1, tail)
-    def _(step):
-        main_step(step, True)
-
-    weight_step(last - 1, 0, False)
-    weight_step(last - 1, 1, False)
-    project(chip, [last - 1])
-    share(chip)
-    pass_wait(tail + 1)
-    sum_step(1, tail + 1)
-    for step in range(tail + 2, last):
-        far_pass(step)
-    for other in far_chips:
-        project(other, [tail, tail + 1])
-    sum_step(0, tail)
-    far_pass(last)
-    for step in range(tail + 2, dp_count):
-        pass_wait(step)
-    for other in far_chips:
-        project(other, list(range(tail + 2, dp_count)))
-        share(other)
-
-    rest = list(range(tail + 2, last))
+        project(other, [middle - 1, middle - 2])
+
+    turns = grad_order[2:last]
+    ops = [(1, turns[0]), (1, turns[1])]
+    for number in range(2, len(turns)):
+        ops += [(0, turns[number - 2]), (1, turns[number])]
+    ops[-2], ops[-1] = ops[-1], ops[-2]
+    ops += [(0, turns[-2]), (0, turns[-1])]
+    ops_left = len(ops)
     order = [(mate_chip + away) % chip_count for away in range(chip_count)]
-    pieces = [block_of(owner, part) for owner in order for part in range(chip_blocks)]
-    per = -(-len(pieces) // max(len(rest), 1))
-    for place_in, step in enumerate(rest):
-        sum_step(1, step)
-        sum_step(0, step - 1)
-        for block in pieces[place_in * per : (place_in + 1) * per]:
-            backward(block)
-    for block in pieces[len(rest) * per :]:
-        backward(block)
+    pending = []
+    for slot, step in ops:
+        sum_step(slot, step)
+        ops_left -= 1
+        if slot == 1:
+            pending.append(step)
+            if passing and not (ops_left > 2 and len(passing) == 2 and len(pending) == 1):
+                pass_next()
+        if len(pending) > 1 and ops_left > 2:
+            for other in far_chips:
+                project(other, pending)
+            pending = []
+        if ops_left == 2:
+            pass_wait_once(last)
+            for other in far_chips:
+                project(other, pending + [last])
+                share(other)
+        if ops_left == 1:
+            for part in range(chip_blocks):
+                backward(block_of(order[0], part))
+            sum_final(1)
+    for owner in order[1:]:
+        for part in range(chip_blocks):
+            backward(block_of(owner, part))
     kv_copy.start()
-    sum_final(1)
-    sum_step(0, last - 1)
     mine = pl.ds(pl.multiple_of(core * half_rows, half_rows), half_rows)
     kv_copy.wait()
     kv_done[...] = (kv_grads[:, mine] + kv_in[...]).astype(jnp.bfloat16)

time: 96.4 us -> 90.6 us (0.940)
  Pallas kernels: 95.4 us -> 89.6 us
    pallas_call x1, Pallas kernels: 94.2 us -> 88.3 us  [shards(): pl.pallas_call(functools.partial(exchange_kernel, dp_count, tensor_count)...]
where the time goes in v3:
time: 90.6 us; the launch traced here: 90.4 us
  Pallas kernels  89.6 us (99%)
    pallas_call x1, Pallas kernels, shards(): pl.pallas_call(functools.partial(exchange_kernel, dp_count, tensor_count)...  88.3 us

profile of v3, /device:TPU:0, one launch (start us, length us, event | category | flops | bytes accessed | tf_op | source)
XLA Modules:
  0.0 90.4 jit_solution(15104162412739545660)
XLA Ops:
  0.6 88.3 %exchange.1 = (bf16[1024,256]{1,0:T(8,128)(2,1)S(1)}, bf16[512,128]{1,0:T(8,128)(2,1)S(1)}, bf16[512,128]{1,0:T(8,128)(2,1)S(1)}, f32[256,1024]{1,0:T(8,128)S(1)}) custom-call(bf16[256,8192]{1,0:T(8,128)(2,1)} %bitcast.7, bf16[256,1024]{1,0:T(8,128)(2,1)} %weight_ref.1, bf16[1024,256]{1,0:T(8,128)(2,1)} %bitcast.8, bf16[1024,256]{1,0:T(8,128)(2,1)} %bitcast.9, ...), custom_call_target="tpu_custom_call" | custom-call | tf_op jit(solution)/shard_map/exchange/pallas_call | solution.py:614
  89.0 1.3 %finish.1 = (bf16[1024,256]{1,0:T(8,128)(2,1)}, bf16[512,128]{1,0:T(8,128)(2,1)}, bf16[512,128]{1,0:T(8,128)(2,1)}, f32[256,1024]{1,0:T(8,128)}) custom-call(bf16[1024,256]{1,0:T(8,128)(2,1)S(1)} %get-tuple-element.12.refs_0_, bf16[512,128]{1,0:T(8,128)(2,1)S(1)} %get-tuple-element.13.refs_1_, bf16[512,128]{1,0:T(8,128)(2,1)S(1)} %get-tuple-element.14.refs_2_, ...), custom_call_target="tpu_custom_call" | custom-call | tf_op jit(solution)/shard_map/finish/pallas_call | solution.py:589

commit v4 on v3

--- a/solution.py
+++ b/solution.py
@@ -37,7 +37,7 @@
     query_full,
     key_full,
     value_full,
-    lengths_ref,
+    lengths_full,
     query_grad_out,
     key_grad_out,
     value_grad_out,
@@ -63,6 +63,7 @@
     kv_grads,
     kv_in,
     kv_done,
+    lengths_ref,
     own_sem,
     own_weight_sem,
     near_send,
@@ -209,7 +210,7 @@
             source,
             weights.at[side, step, slots[slot]],
             weight_send,
-            weight_recv.at[side, step, slot],
+            weight_recv.at[hop_step(hop, minor), slot],
             ring[1 - side if minor else side],
             tensor_index,
         )
@@ -219,7 +220,7 @@
             sums_out.at[side, step, slots[slot]],
             sums_in.at[side, step, slots[slot]],
             sum_send,
-            sum_recv.at[side, step, slot],
+            sum_recv.at[step, slot],
             ring[side if step >= middle - 1 else 1 - side],
             tensor_index,
         )
@@ -260,19 +261,19 @@
         partner,
     )
 
-    loads = [
-        pltpu.make_async_copy(query_full, query_ref, load_sem.at[0]),
-        pltpu.make_async_copy(key_full.at[:, kv_columns], key_ref, load_sem.at[1]),
-        pltpu.make_async_copy(value_full.at[:, kv_columns], value_ref, load_sem.at[2]),
-    ]
-    for load in loads:
-        load.start()
-
     targets = [(dp_index, partner), (ring[0], tensor_index), (ring[1], tensor_index)]
     targets += [(dp_index, other * 2 + core) for other in far_chips]
     barrier = pltpu.get_barrier_semaphore()
     for target in targets:
         pl.semaphore_signal(barrier, inc=1, device_id=target, device_id_type=MESH)
+    loads = [
+        pltpu.make_async_copy(query_full, query_ref, load_sem.at[0]),
+        pltpu.make_async_copy(key_full.at[:, kv_columns], key_ref, load_sem.at[1]),
+        pltpu.make_async_copy(value_full.at[:, kv_columns], value_ref, load_sem.at[2]),
+        pltpu.make_async_copy(lengths_full, lengths_ref, load_sem.at[3]),
+    ]
+    for load in loads:
+        load.start()
     pl.semaphore_wait(barrier, len(targets))
 
     def far_start(step):
@@ -290,15 +291,6 @@
     for side in (0, 1):
         weight_copy(side, 1, 1, 0).start()
     far_start(grad_order[0])
-    for side in (0, 1):
-        own_weight(side).start()
-
-    @pl.loop(0, dp_count)
-    def _(step):
-        for side in (0, 1):
-            near_copy(side, step).start()
-            own_copy(side, step).start()
-
     nt = (((1,), (1,)), ((), ()))
     tn = (((0,), (0,)), ((), ()))
 
@@ -401,9 +393,10 @@
         drain(weights.at[:, last, slots[0]], own_weight_sem)
 
     def weight_step(hop, minor, slot):
-        for side in (0, 1):
-            weight_copy(side, hop, minor, slot).wait_recv()
-            if hop + minor < middle:
+        step = hop_step(hop, minor)
+        drain(weights.at[:, step, slots[slot]], weight_recv.at[step, slot])
+        if hop + minor < middle:
+            for side in (0, 1):
                 weight_copy(side, hop + 1, minor, slot).start()
 
     def far_pass(step):
@@ -423,6 +416,7 @@
     def pass_wait_once(step):
         if step not in passed:
             passed.add(step)
+            waiting.append(step)
             pass_wait(step)
 
     def sum_part(slot, side, step):
@@ -435,7 +429,8 @@
         for side in (0, 1):
             part = sum_part(slot, side, step)
             if not first:
-                sum_copy(side, before, slot).wait_recv()
+                if side == 0:
+                    drain(sums_in.at[:, before, slots[slot]], sum_recv.at[before, slot])
                 part = part + sums_in[side, before, slots[slot]].astype(jnp.float32)
             sums_out[side, step, slots[slot]] = part.astype(jnp.bfloat16)
             sum_copy(side, step, slot).start()
@@ -451,7 +446,8 @@
         for side in (0, 1):
             part = sum_part(slot, side, last)
             for before in (0, last - 1):
-                sum_copy(side, before, slot).wait_recv()
+                if side == 0:
+                    drain(sums_in.at[:, before, slots[slot]], sum_recv.at[before, slot])
                 part = part + sums_in[side, before, slots[slot]].astype(jnp.float32)
             if slot == 0:
                 weight_grad_ref[0, side] = part
@@ -463,7 +459,17 @@
     for load in loads:
         load.wait()
     blocks = seq_len // forward_rows
-    for index in range(blocks - 1):
+    forward(0)
+
+    @pl.loop(0, dp_count)
+    def _(step):
+        for side in (0, 1):
+            near_copy(side, step).start()
+            own_copy(side, step).start()
+
+    for side in (0, 1):
+        own_weight(side).start()
+    for index in range(1, blocks - 1):
         forward(index)
     weight_step(1, 0, 0)
     forward(blocks - 1)
@@ -480,64 +486,65 @@
     local_wait()
     project(chip, [last])
     passing = list(grad_order)
+    waiting = []
 
     def pass_next():
         far_pass(passing.pop(0))
 
-    for hop in range(2, middle + 1):
+    def far_project(steps):
+        for other in far_chips:
+            project(other, steps)
+        waiting[:] = [step for step in waiting if step not in steps]
+
+    for hop in range(2, middle):
         weight_step(hop, 0, 0)
+        if hop == middle - 1:
+            outs_copy.wait_recv()
+            sum_step(1, grad_order[0])
         weight_step(hop - 1, 0, 1)
+        if hop == middle - 1:
+            pass_next()
+            sum_step(0, grad_order[1])
+            sum_step(1, grad_order[1])
         weight_step(hop - 1, 1, 1)
-        if hop < middle:
-            weight_step(hop, 1, 0)
+        weight_step(hop, 1, 0)
         if hop == middle - 2:
             pass_next()
         project(chip, [hop - 2, last + 1 - hop])
         if hop == middle - 2:
-            sum_step(0, middle - 1)
-        if hop == middle - 1:
-            outs_copy.wait_recv()
-            sum_step(1, middle - 1)
+            sum_step(0, grad_order[0])
+    pass_next()
+    sum_step(1, grad_order[2])
+    weight_step(middle, 0, 0)
+    pass_next()
+    sum_step(1, grad_order[3])
+    weight_step(middle - 1, 0, 1)
+    pass_next()
+    weight_step(middle - 1, 1, 1)
+    project(chip, [middle - 2, middle])
+    far_project(grad_order[1:4])
+
+    order = [(mate_chip + away) % chip_count for away in range(chip_count)]
+    for number in range(4, last):
+        if number == 6:
+            weight_step(middle, 0, 1)
+            project(chip, [middle - 1])
+            share(chip)
             pass_next()
-    sum_step(0, middle - 2)
-    weight_step(middle, 0, 1)
-    sum_step(1, middle - 2)
-    pass_next()
-    pass_next()
-    project(chip, [middle - 1])
-    share(chip)
+            far_project(list(waiting))
+        sum_step(1, grad_order[number])
+        if number != 5:
+            pass_next()
+        sum_step(0, grad_order[number - 2])
+    pass_wait_once(last)
+    far_project(list(waiting))
     for other in far_chips:
-        project(other, [middle - 1, middle - 2])
-
-    turns = grad_order[2:last]
-    ops = [(1, turns[0]), (1, turns[1])]
-    for number in range(2, len(turns)):
-        ops += [(0, turns[number - 2]), (1, turns[number])]
-    ops[-2], ops[-1] = ops[-1], ops[-2]
-    ops += [(0, turns[-2]), (0, turns[-1])]
-    ops_left = len(ops)
-    order = [(mate_chip + away) % chip_count for away in range(chip_count)]
-    pending = []
-    for slot, step in ops:
-        sum_step(slot, step)
-        ops_left -= 1
-        if slot == 1:
-            pending.append(step)
-            if passing and not (ops_left > 2 and len(passing) == 2 and len(pending) == 1):
-                pass_next()
-        if len(pending) > 1 and ops_left > 2:
-            for other in far_chips:
-                project(other, pending)
-            pending = []
-        if ops_left == 2:
-            pass_wait_once(last)
-            for other in far_chips:
-                project(other, pending + [last])
-                share(other)
-        if ops_left == 1:
-            for part in range(chip_blocks):
-                backward(block_of(order[0], part))
-            sum_final(1)
+        share(other)
+    sum_step(0, grad_order[last - 2])
+    for part in range(chip_blocks):
+        backward(block_of(order[0], part))
+    sum_final(1)
+    sum_step(0, grad_order[last - 1])
     for owner in order[1:]:
         for part in range(chip_blocks):
             backward(block_of(owner, part))
@@ -619,8 +626,7 @@
             kv_shape,
             pltpu.VMEM((depth, width), full),
         ),
-        in_specs=[pl.BlockSpec(memory_space=pltpu.HBM)] * 5
-        + [pl.BlockSpec(memory_space=pltpu.SMEM)],
+        in_specs=[pl.BlockSpec(memory_space=pltpu.HBM)] * 6,
         out_specs=(anywhere,) * 4,
         scratch_shapes=[
             pltpu.VMEM((2, dp_count, seq_len, quarter), low),
@@ -644,6 +650,7 @@
             pltpu.VMEM((2, seq_len, HEAD_SIZE), full),
             pltpu.VMEM((2, seq_len // 2, HEAD_SIZE), full),
             pltpu.VMEM((2, seq_len // 2, HEAD_SIZE), low),
+            pltpu.SMEM(doc_lengths.shape, jnp.int32),
             dma,
             dma,
             dma,
@@ -655,9 +662,9 @@
             dma,
             dma((2,)),
             dma,
-            dma((2, dp_count - 1, 2)),
-            dma,
-            dma((2, dp_count - 1, 2)),
+            dma((dp_count - 1, 2)),
+            dma,
+            dma((dp_count - 1, 2)),
             dma,
             dma,
             dma,
@@ -666,7 +673,7 @@
             dma((2,)),
             dma,
             dma,
-            dma((3,)),
+            dma((4,)),
             dma,
             dma,
             dma((2,)),

time: 90.6 us -> 89.1 us (0.983)
  Pallas kernels: 89.6 us -> 88.1 us
    pallas_call x1, Pallas kernels: 88.3 us -> 86.9 us  [shards(): pl.pallas_call(functools.partial(exchange_kernel, dp_count, tensor_count)...]
where the time goes in v4:
time: 89.1 us; the launch traced here: 88.9 us
  Pallas kernels  88.1 us (99%)
    pallas_call x1, Pallas kernels, shards(): pl.pallas_call(functools.partial(exchange_kernel, dp_count, tensor_count)...  86.9 us

profile of v4, /device:TPU:0, one launch (start us, length us, event | category | flops | bytes accessed | tf_op | source)
XLA Modules:
  0.0 88.9 jit_solution(3465200249413384995)
XLA Ops:
  0.6 86.9 %exchange.1 = (bf16[1024,256]{1,0:T(8,128)(2,1)S(1)}, bf16[512,128]{1,0:T(8,128)(2,1)S(1)}, bf16[512,128]{1,0:T(8,128)(2,1)S(1)}, f32[256,1024]{1,0:T(8,128)S(1)}) custom-call(bf16[256,8192]{1,0:T(8,128)(2,1)} %bitcast.7, bf16[256,1024]{1,0:T(8,128)(2,1)} %weight_ref.1, bf16[1024,256]{1,0:T(8,128)(2,1)} %bitcast.8, bf16[1024,256]{1,0:T(8,128)(2,1)} %bitcast.9, ...), custom_call_target="tpu_custom_call" | custom-call | tf_op jit(solution)/shard_map/exchange/pallas_call | solution.py:621
  87.5 1.3 %finish.1 = (bf16[1024,256]{1,0:T(8,128)(2,1)}, bf16[512,128]{1,0:T(8,128)(2,1)}, bf16[512,128]{1,0:T(8,128)(2,1)}, f32[256,1024]{1,0:T(8,128)}) custom-call(bf16[1024,256]{1,0:T(8,128)(2,1)S(1)} %get-tuple-element.12.refs_0_, bf16[512,128]{1,0:T(8,128)(2,1)S(1)} %get-tuple-element.13.refs_1_, bf16[512,128]{1,0:T(8,128)(2,1)S(1)} %get-tuple-element.14.refs_2_, ...), custom_call_target="tpu_custom_call" | custom-call | tf_op jit(solution)/shard_map/finish/pallas_call | solution.py:596

commit v5 on v4

v5 whole, which is shorter than its diff:
```python
import functools

import jax
import jax.numpy as jnp
from jax import lax
from jax.experimental import pallas as pl
from jax.experimental.pallas import tpu as pltpu
from jax.sharding import PartitionSpec as P

HEAD_SIZE = 128


MESH = pl.DeviceIdType.MESH


def block_sizes(seq_len, tensor_count):
    rows = seq_len // tensor_count
    forward_rows = min(256, seq_len)
    part_rows = rows // max(1, rows // 128)
    block_rows = max(part_rows, min(128, 2 * rows))
    return forward_rows, part_rows, block_rows, seq_len // 2 + forward_rows


def exchange_kernel(
    dp_count,
    tensor_count,
    grad_ref,
    weight_ref,
    query_full,
    key_full,
    value_full,
    lengths_full,
    query_grad_out,
    key_grad_out,
    value_grad_out,
    weight_grad_out,
    grads,
    weights,
    sums_out,
    sums_in,
    cross_out,
    cross_in,
    accum,
    query_ref,
    key_ref,
    value_ref,
    query_grad_ref,
    weight_grad_ref,
    probs,
    probs_t,
    outs,
    outs_own,
    outs_t,
    share_out,
    share_in,
    turn_out,
    out_grad,
    back_out,
    back_in,
    kv_grads,
    kv_in,
    kv_done,
    lengths_ref,
    own_sem,
    near_send,
    near_recv,
    far_send,
    far_recv,
    pass_send,
    pass_recv,
    line_send,
    line_recv,
    total_recv,
    wing_send,
    wing_recv,
    cross_send,
    cross_recv,
    outs_send,
    outs_recv,
    share_send,
    share_recv,
    turn_send,
    turn_recv,
    back_send,
    back_recv,
    kv_send,
    kv_recv,
    load_sem,
    query_sem,
    put_sem,
    kv_sem,
):
    dp_index = lax.axis_index("dp")
    tensor_index = lax.axis_index("tensor")
    chip_count = tensor_count // 2
    pairs = chip_count // 2
    spots = dp_count // 2
    chip, core = tensor_index // 2, tensor_index % 2
    pair, parity = chip // 2, chip % 2
    mate = (pair * 2 + 1 - parity) * 2 + core
    partner = chip * 2 + 1 - core
    spot, lane = dp_index // 2, dp_index % 2
    twin = spot * 2 + 1 - lane
    rows = grad_ref.shape[0]
    depth, width = weight_ref.shape
    half = width // 2
    seq_len = query_full.shape[0]
    heads = depth // HEAD_SIZE
    half_rows = seq_len // 2
    score_scale = HEAD_SIZE ** (-0.5)
    forward_rows, part_rows, back_rows, window = block_sizes(seq_len, tensor_count)
    kv_columns = pl.ds(pl.multiple_of(tensor_index // 2 * HEAD_SIZE, HEAD_SIZE), HEAD_SIZE)
    slots = (slice(0, depth), slice(depth, 2 * depth))
    sides = (slice(0, half), slice(half, width))
    chunks = ((0, 0), (0, 1), (1, 0))
    ways = (1, -1)
    routes = [(away, whose) for whose in (1, 0) for away in range(pairs) if away or whose]
    fars = len(routes)
    pieces = rows // part_rows

    def exists(way):
        return spot <= spots - 2 if way > 0 else spot >= 1

    def reaches(way, far):
        return spot + far <= spots - 1 if way > 0 else spot >= far

    def local_rows(whose, which_pair, which_core):
        start = ((whose * pairs + which_pair) * 2 + which_core) * rows
        return pl.ds(pl.multiple_of(start, rows), rows)

    def columns(which_lane, block, side):
        start = (2 * block + which_lane) * width + side * half
        return pl.ds(pl.multiple_of(start, half), half)

    def remote(source, target, send, recv, dp_to, tensor_to):
        return pltpu.make_async_remote_copy(
            source, target, send, recv, device_id=(dp_to, tensor_to), device_id_type=MESH
        )

    def drain(ref, sem):
        pltpu.make_async_copy(ref, ref, sem).wait()

    def own_copy(side, block):
        return pltpu.make_async_copy(
            grad_ref.at[:, columns(lane, block, side)],
            grads.at[side, block, local_rows(0, pair, core)],
            own_sem.at[0],
        )

    def own_weight(side):
        return pltpu.make_async_copy(
            weight_ref.at[:, sides[side]], weights.at[side, spot, slots[0]], own_sem.at[1]
        )

    def near_copy(side, block):
        return remote(
            grad_ref.at[:, columns(lane, block, side)],
            grads.at[side, block, local_rows(0, pair, core)],
            near_send,
            near_recv,
            dp_index,
            partner,
        )

    def far_copy(route, side, block):
        away, whose = routes[route]
        return remote(
            grad_ref.at[:, columns(1 - lane if whose else lane, block, side)],
            grads.at[side, block, local_rows(whose, pair, core)],
            far_send.at[route],
            far_recv.at[route, block],
            twin if whose else dp_index,
            ((pair + away) % pairs * 2 + parity) * 2 + core,
        )

    def source_rows(route, which_core):
        away, whose = routes[route]
        return local_rows(whose, (pair + pairs - away) % pairs, which_core)

    def pass_copy(route, side, block):
        piece = grads.at[side, block, source_rows(route, core)]
        return remote(
            piece, piece, pass_send.at[route], pass_recv.at[route, block], dp_index, partner
        )

    def piece_rows(rows_slice, piece):
        return pl.ds(
            pl.multiple_of(rows_slice.start + piece * part_rows, part_rows), part_rows
        )

    def last_copy(route, piece):
        away, whose = routes[route]
        return remote(
            grad_ref.at[
                slice(piece * part_rows, (piece + 1) * part_rows),
                columns(1 - lane if whose else lane, spot, 0),
            ],
            grads.at[0, spot, piece_rows(local_rows(whose, pair, core), piece)],
            far_send.at[route],
            far_recv.at[route, spots + piece],
            twin if whose else dp_index,
            ((pair + away) % pairs * 2 + parity) * 2 + core,
        )

    def last_pass_copy(route, piece):
        here = grads.at[0, spot, piece_rows(source_rows(route, core), piece)]
        return remote(
            here,
            here,
            pass_send.at[route],
            pass_recv.at[route, spots + piece],
            dp_index,
            partner,
        )

    def line_copy(way, far, chunk):
        side, slot = chunks[chunk]
        block = spot - way * far
        if far == 0 and slot == 0:
            source = weight_ref.at[:, sides[side]]
        else:
            source = weights.at[side, block, slots[slot]]
        return remote(
            source,
            weights.at[side, block, slots[slot]],
            line_send.at[(1 - way) // 2],
            line_recv.at[chunk, block],
            dp_index + 2 * way,
            tensor_index,
        )

    def wing_copy(block, side=1, own=False):
        return remote(
            weight_ref.at[:, sides[side]] if own else weights.at[side, block, slots[0]],
            weights.at[side, block, slots[1]],
            wing_send,
            wing_recv.at[block if side else spots],
            dp_index,
            mate,
        )

    def total_copy(way, far, chunk):
        owner = spot + way * far
        index = spots if way < 0 and far == 1 else owner
        return remote(
            sums_out.at[chunk, owner],
            sums_in.at[chunk, index],
            line_send.at[(1 - way) // 2],
            total_recv.at[chunk, index],
            dp_index + 2 * way,
            tensor_index,
        )

    def cross_copy(block):
        return remote(
            cross_out.at[block],
            cross_in.at[block],
            cross_send,
            cross_recv.at[block],
            dp_index,
            mate,
        )

    def chip_lanes(which_pair, which_parity):
        start = (2 * which_pair + which_parity) * 2 * rows
        return pl.ds(pl.multiple_of(start, 2 * rows), 2 * rows)

    def outs_copy(kind, which_pair):
        here = slice(which_pair * 2 * rows, (which_pair + 1) * 2 * rows)
        there = slice(half_rows + which_pair * 2 * rows, half_rows + (which_pair + 1) * 2 * rows)
        own = outs_own.at[:, chip_lanes(which_pair, parity)]
        if kind == 0:
            return pltpu.make_async_copy(own, outs_t.at[0, :, here], own_sem.at[2])
        if kind == 1:
            other = outs_own.at[:, chip_lanes(which_pair, 1 - parity)]
            return remote(
                other, outs_t.at[1, :, here], outs_send.at[0], outs_recv.at[0], dp_index, mate
            )
        if kind == 2:
            return remote(
                own, outs_t.at[0, :, there], outs_send.at[1], outs_recv.at[1], twin, tensor_index
            )
        return remote(
            outs_t.at[1, :, here],
            outs_t.at[1, :, there],
            outs_send.at[2],
            outs_recv.at[2],
            twin,
            tensor_index,
        )

    parts = [
        (which_pair, which_core, piece)
        for piece in range(rows // part_rows)
        for which_pair in range(pairs)
        for which_core in (0, 1)
    ]

    def part_start(part):
        which_pair, which_core, piece = parts[part]
        return (which_pair * 2 + which_core) * rows + piece * part_rows

    def part_slice(part):
        return slice(part_start(part), part_start(part) + part_rows)

    def share_copy(part):
        here = part_slice(part)
        return remote(
            share_out.at[here],
            share_in.at[here],
            share_send,
            share_recv.at[part],
            twin,
            tensor_index,
        )

    def turn_copy(part):
        here = part_slice(part)
        return remote(
            turn_out.at[here], out_grad.at[1, here], turn_send, turn_recv.at[part], dp_index, mate
        )

    def back_copy(part):
        here = slice(part * (depth // len(parts)), (part + 1) * (depth // len(parts)))
        return remote(back_out.at[here], back_in.at[here], back_send, back_recv, dp_index, mate)

    kv_copy = remote(
        kv_grads.at[:, pl.ds(pl.multiple_of((1 - core) * half_rows, half_rows), half_rows)],
        kv_in,
        kv_send,
        kv_recv,
        dp_index,
        partner,
    )

    targets = [(dp_index, partner), (dp_index, mate), (twin, tensor_index)]
    for away in range(1, pairs):
        other = ((pair + away) % pairs * 2 + parity) * 2 + core
        targets += [(dp_index, other), (twin, other)]
    barrier = pltpu.get_barrier_semaphore()
    for target in targets:
        pl.semaphore_signal(barrier, inc=1, device_id=target, device_id_type=MESH)
    for way in ways:

        @pl.when(exists(way))
        def _():
            pl.semaphore_signal(
                barrier,
                inc=1,
                device_id=(dp_index + 2 * way, tensor_index),
                device_id_type=MESH,
            )

    loads = [
        pltpu.make_async_copy(query_full, query_ref, load_sem.at[0]),
        pltpu.make_async_copy(key_full.at[:, kv_columns], key_ref, load_sem.at[1]),
        pltpu.make_async_copy(value_full.at[:, kv_columns], value_ref, load_sem.at[2]),
        pltpu.make_async_copy(lengths_full, lengths_ref, load_sem.at[3]),
    ]
    for load in loads:
        load.start()
    beside = (spot + spots - 2) // (spots - 1) + (2 * spots - 3 - spot) // (spots - 1)
    pl.semaphore_wait(barrier, len(targets) + beside)

    upper = (2 * spot) // spots
    first_block = (1 - upper) * (spots - 1)

    def far_start(block):
        for side in (0, 1):
            for route in range(fars):
                far_copy(route, side, block).start()

    def line_start(chunk):
        for way in ways:

            @pl.when(exists(way))
            def _():
                line_copy(way, 0, chunk).start()

    line_start(2)
    wing_copy(spot, 0, True).start()
    far_start(first_block)
    line_start(0)
    nt = (((1,), (1,)), ((), ()))
    tn = (((0,), (0,)), ((), ()))

    def dot(left, right, dims):
        return lax.dot_general(left, right, dims, preferred_element_type=jnp.float32)

    def window_start(index):
        skip, total = half_rows // forward_rows, seq_len // forward_rows
        past = (index + total - skip) // total
        return past * (index - skip) * forward_rows

    def window_keys(index):
        return pl.ds(pl.multiple_of(window_start(index), forward_rows), window)

    def forward(index):
        here = pl.ds(pl.multiple_of(index * forward_rows, forward_rows), forward_rows)
        query_places = index * forward_rows + lax.broadcasted_iota(jnp.int32, (forward_rows, 1), 0)
        key_places = window_start(index) + lax.broadcasted_iota(
            jnp.int32, (forward_rows, window), 1
        )
        doc_start = jnp.zeros((forward_rows, 1), jnp.int32)
        doc_end = jnp.int32(0)
        for doc in range(lengths_ref.shape[1]):
            doc_end = doc_end + lengths_ref[0, doc]
            doc_start = jnp.where(query_places >= doc_end, doc_end, doc_start)
        allowed = (key_places >= doc_start) & (key_places <= query_places)
        keys, values = key_ref[window_keys(index)], value_ref[window_keys(index)]
        for head in range(heads):
            lanes = slice(head * HEAD_SIZE, (head + 1) * HEAD_SIZE)
            scores = dot(query_ref[here, lanes], keys, nt) * score_scale
            scores = jnp.where(allowed, scores, -jnp.inf)
            row_max = jnp.max(scores, axis=1, keepdims=True)
            total = jnp.sum(jnp.exp(scores - row_max), axis=1, keepdims=True)
            prob = jnp.exp(scores - (row_max + jnp.log(total)))
            probs[head, here] = prob
            out = jnp.dot(prob.astype(jnp.bfloat16), values, preferred_element_type=jnp.float32)
            outs[here, lanes] = out.astype(jnp.bfloat16)
            outs_own[lanes, here] = out.T.astype(jnp.bfloat16)
            for part in range(forward_rows // back_rows):
                piece = prob[part * back_rows : (part + 1) * back_rows]
                block = index * (forward_rows // back_rows) + part
                probs_t[head, block] = piece.T.astype(jnp.bfloat16)

    def backward(which, start):
        whose = parity if which == 0 else 1 - parity
        place = start // (2 * rows) * 4 * rows + start % (2 * rows)
        block = place // back_rows + whose * (2 * rows // back_rows)
        here = pl.ds(pl.multiple_of(block * back_rows, back_rows), back_rows)
        seen = window_keys(block // (forward_rows // back_rows))
        keys, values = key_ref[seen], value_ref[seen]
        key_total, value_total = kv_grads[0, seen], kv_grads[1, seen]
        for head in range(heads):
            lanes = slice(head * HEAD_SIZE, (head + 1) * HEAD_SIZE)
            grad = out_grad[which, start : start + back_rows, lanes]
            delta = jnp.sum(
                grad.astype(jnp.float32) * outs[here, lanes].astype(jnp.float32), axis=1, keepdims=True
            )
            dscore = probs[head, here] * (dot(grad, values, nt) - delta) * score_scale
            dscore = dscore.astype(jnp.bfloat16)
            query_grad_ref[here, lanes] = jnp.dot(
                dscore, keys, preferred_element_type=jnp.float32
            ).astype(jnp.bfloat16)
            key_total += dot(dscore, query_ref[here, lanes], tn)
            value_total += jnp.dot(probs_t[head, block], grad, preferred_element_type=jnp.float32)
        kv_grads[0, seen] = key_total
        kv_grads[1, seen] = value_total
        pltpu.make_async_copy(
            query_grad_ref.at[here], query_grad_out.at[here], query_sem
        ).start()

    def project(block, whose, which=(0, 1), piece=None):
        if piece is None:
            areas = [slice(whose * half_rows, (whose + 1) * half_rows)]
        else:
            areas = [
                slice(half_rows + part_start(part), half_rows + part_start(part) + part_rows)
                for part in range(len(parts))
                if parts[part][2] == piece
            ]
        for here in areas:
            total = accum[here]
            for side in which:
                total += dot(grads[side, block, here], weights[side, block], nt)
            accum[here] = total

    def line_hop(far, chunk):
        side, slot = chunks[chunk]
        for way in ways:

            @pl.when(reaches(-way, far))
            def _():
                block = spot - way * far
                drain(weights.at[side, block, slots[slot]], line_recv.at[chunk, block])

                @pl.when(exists(way))
                def _():
                    line_copy(way, far, chunk).start()

                if chunk == 2:
                    wing_copy(block).start()

    def wing_wait(block, side=1):
        drain(weights.at[side, block, slots[1]], wing_recv.at[block if side else spots])

    def hop_project(far):
        for way in ways:

            @pl.when(reaches(-way, far))
            def _():
                wing_wait(spot - way * far)
                project(spot - way * far, 0)

    def far_pass(block, which=(0, 1)):
        for route in range(fars):
            for side in which[:1] if len(which) == 1 else ():
                drain(grads.at[side, block, source_rows(route, core)], far_recv.at[route, block])
            if len(which) == 2:
                drain(grads.at[:, block, source_rows(route, core)], far_recv.at[route, block])
            for side in which:
                pass_copy(route, side, block).start()

    def pass_wait(block, which=(0, 1)):
        for route in range(fars):
            there = source_rows(route, 1 - core)
            if len(which) == 2:
                drain(grads.at[:, block, there], pass_recv.at[route, block])
            else:
                drain(grads.at[which[0], block, there], pass_recv.at[route, block])

    def last_pass(piece):
        for route in range(fars):
            here = piece_rows(source_rows(route, core), piece)
            drain(grads.at[0, spot, here], far_recv.at[route, spots + piece])
            last_pass_copy(route, piece).start()

    def last_wait(piece):
        for route in range(fars):
            here = piece_rows(source_rows(route, 1 - core), piece)
            drain(grads.at[0, spot, here], pass_recv.at[route, spots + piece])

    def sum_part(slot, side, block):
        return jnp.dot(outs_t[slot], grads[side, block], preferred_element_type=jnp.float32)

    def cross(block):
        cross_out[block] = sum_part(1, 1, block).astype(jnp.bfloat16)
        cross_copy(block).start()

    def owner_do(far, work):
        for way in ways:

            @pl.when(reaches(way, far))
            def _():
                work(way, spot + way * far)

    def total_sum(chunk, owner):
        side, slot = chunks[chunk]
        part = sum_part(slot, side, owner) + sums_in[chunk, owner].astype(jnp.float32)
        if side:
            drain(cross_in.at[owner], cross_recv.at[owner])
            part = part + cross_in[owner].astype(jnp.float32)
        sums_out[chunk, owner] = part.astype(jnp.bfloat16)

    def total_step(far, chunk):
        def work(way, owner):
            @pl.when(owner != first_block)
            def _():
                @pl.when(exists(-way))
                def _():
                    drain(sums_in.at[chunk, owner], total_recv.at[chunk, owner])

                total_sum(chunk, owner)
                total_copy(way, far, chunk).start()

        owner_do(far, work)

    def total_first(chunk, at_end):
        edge = spot % (spots - 1)

        @pl.when(edge == 0 if at_end else edge != 0)
        def _():
            if not at_end:
                drain(sums_in.at[chunk, first_block], total_recv.at[chunk, first_block])
            total_sum(chunk, first_block)
            remote(
                sums_out.at[chunk, first_block],
                sums_in.at[chunk, first_block],
                line_send.at[upper],
                total_recv.at[chunk, first_block],
                dp_index + 2 - 4 * upper,
                tensor_index,
            ).start()

    def total_final(chunk):
        side, slot = chunks[chunk]
        part = sum_part(slot, side, spot)
        if side:
            drain(cross_in.at[spot], cross_recv.at[spot])
            part = part + cross_in[spot].astype(jnp.float32)
        for way, index in ((-1, spot), (1, spots)):

            @pl.when(exists(way))
            def _():
                drain(sums_in.at[chunk, index], total_recv.at[chunk, index])

            part = part + sums_in[chunk, index].astype(jnp.float32)
        return part

    def weight_put(side):
        return pltpu.make_async_copy(
            weight_grad_ref.at[side], weight_grad_out.at[:, sides[side]], put_sem
        )

    def share(piece):
        for part in range(len(parts)):
            if parts[part][2] == piece:
                here = part_slice(part)
                there = slice(half_rows + here.start, half_rows + here.stop)
                share_out[here] = accum[there].astype(jnp.bfloat16)
                share_copy(part).start()

    def settle(part):
        here = part_slice(part)
        share_copy(part).wait_recv()
        both = (accum[here] + share_in[here].astype(jnp.float32)).astype(jnp.bfloat16)
        turn_out[here] = both[:, slots[1]]
        turn_copy(part).start()
        out_grad[0, here] = both[:, slots[0]]

    def finished(part):
        start = part_start(part)
        if back_rows == part_rows:
            return start
        return start - rows if parts[part][1] == 1 else None

    for load in loads:
        load.wait()
    blocks = seq_len // forward_rows
    forward(0)

    @pl.loop(0, spots)
    def _(block):
        for side in (0, 1):
            near_copy(side, block).start()
            own_copy(side, block).start()

    for side in (0, 1):
        own_weight(side).start()
    for index in range(1, blocks):
        forward(index)
    for which_pair in range(pairs):
        outs_copy(1, which_pair).start()
        outs_copy(2, which_pair).start()
        outs_copy(0, which_pair).start()
    wing_copy(spot, 1, True).start()
    line_hop(1, 2)
    wing_wait(spot, 0)
    line_start(1)
    line_hop(1, 0)

    accum[...] = jnp.zeros_like(accum)
    kv_grads[...] = jnp.zeros_like(kv_grads)
    for way in ways:

        @pl.when(reaches(way, spots - 1))
        def _():
            for chunk in range(3):
                for index in range(spots + 1):
                    if index != (spots if way > 0 else spots - 1):
                        sums_in[chunk, index] = jnp.zeros_like(sums_in[chunk, index])

    drain(grads.at[:, :, local_rows(0, pair, core)], own_sem.at[0])
    drain(weights.at[:, spot, slots[0]], own_sem.at[1])
    drain(outs_t.at[0, :, slice(0, half_rows)], own_sem.at[2])
    drain(grads.at[:, :, local_rows(0, pair, 1 - core)], near_recv)
    def pass_rest(far):
        def work(way, owner):
            @pl.when(owner != first_block)
            def _():
                far_pass(owner)

        owner_do(far, work)

    drain(outs_t.at[1, :, slice(0, half_rows)], outs_recv.at[0])
    for which_pair in range(pairs):
        outs_copy(3, which_pair).start()

    def rest_start(far):
        def work(way, owner):
            if far > 1 or spots == 2:

                @pl.when(owner != first_block)
                def _():
                    far_start(owner)

            else:
                far_start(owner)

        owner_do(far, work)

    for far in range(spots - 1, 0, -1):
        rest_start(far)
    for route in range(fars):
        far_copy(route, 1, spot).start()
    for piece in range(pieces):
        for route in range(fars):
            last_copy(route, piece).start()
    def rest_do(far, work):
        def inner(way, owner):
            @pl.when(owner != first_block)
            def _():
                work(owner)

        owner_do(far, inner)

    def both_project(far):
        owner_do(far, lambda way, owner: project(owner, 1))

    far_pass(first_block)
    drain(outs_t.at[0, :, slice(half_rows, seq_len)], outs_recv.at[1])
    pass_wait(first_block)
    total_first(0, True)
    line_hop(1, 1)
    drain(outs_t.at[1, :, slice(half_rows, seq_len)], outs_recv.at[2])
    cross(first_block)
    total_first(1, True)
    line_hop(2, 2)
    line_hop(2, 0)
    total_first(0, False)
    wing_wait(spot)
    project(spot, 0)
    total_first(2, True)
    total_first(1, False)
    line_hop(2, 1)
    hop_project(1)
    for far in range(spots - 2, 0, -1):
        hop = spots - far + 1
        pass_rest(far)
        rest_do(far, pass_wait)
        rest_do(far, cross)
        total_step(far, 1)
        total_step(far, 0)
        if far == spots - 2:
            total_first(2, False)
            hop_project(2)
        if far <= spots // 2:
            both_project(far)
        if far == 1:
            far_pass(spot, (1,))
            line_hop(spots - 1, 1)
            hop_project(spots - 1)
            both_project(spots - 1)
            pass_wait(spot, (1,))
            cross(spot)
            project(spot, 1, (1,))
            last_pass(0)
        if hop < spots:
            line_hop(hop, 2)
            line_hop(hop, 0)
        if far > 1:
            total_step(far, 2)
        if hop < spots - 1:
            line_hop(hop, 1)
            hop_project(hop)
            if hop > spots // 2:
                both_project(hop)
    for piece in range(pieces):
        last_wait(piece)
        project(spot, 1, (0,), piece)
        share(piece)
        if piece + 1 < pieces:
            last_pass(piece + 1)

    total_step(1, 2)
    back_out[...] = total_final(1).astype(jnp.bfloat16)
    later = []
    for part in range(len(parts)):
        settle(part)
        back_copy(part).start()
        if finished(part) is not None:
            backward(0, finished(part))
        if part == len(parts) - 2:
            weight_grad_ref[0] = total_final(0)
        for earlier in later:
            turn_copy(earlier).wait_recv()
            if finished(earlier) is not None:
                backward(1, finished(earlier))
        later = [part]
    weight_grad_ref[1] = total_final(2)
    weight_put(1).start()
    turn_copy(later[0]).wait_recv()
    backward(1, finished(later[0]))
    kv_copy.start()
    drain(back_in, back_recv)
    weight_grad_ref[0] = weight_grad_ref[0] + back_in[...].astype(jnp.float32)
    weight_put(0).start()
    mine = pl.ds(pl.multiple_of(core * half_rows, half_rows), half_rows)
    kv_copy.wait()
    kv_done[...] = (kv_grads[:, mine] + kv_in[...]).astype(jnp.bfloat16)
    kv_puts = [
        pltpu.make_async_copy(kv_done.at[which], to, kv_sem.at[which])
        for which, to in enumerate((key_grad_out, value_grad_out))
    ]
    for put in kv_puts:
        put.start()

    drain(grads.at[:, :, local_rows(0, pair, core)], near_send)
    for route in range(fars):
        drain(grads.at[:, :, local_rows(0, pair, core)], far_send.at[route])
        drain(grads.at[:, :, local_rows(0, pair, core)], pass_send.at[route])
    for index in range(3):
        drain(outs_t.at[0, :, slice(0, half_rows)], outs_send.at[index])
    drain(share_out, share_send)
    drain(turn_out, turn_send)
    drain(query_grad_ref, query_sem)
    for put in kv_puts:
        put.wait()
    drain(sums_in.at[0], wing_send)
    drain(cross_out, cross_send)
    drain(back_out, back_send)
    for way in ways:

        @pl.when(exists(way))
        def _():
            drain(grads.at[0, :, slice(0, 3 * depth)], line_send.at[(1 - way) // 2])

    drain(weight_grad_ref, put_sem)


def finish_kernel(*refs):
    count = (len(refs) - 1) // 2
    puts = [
        pltpu.make_async_copy(refs[i], refs[count + i], refs[2 * count].at[i]) for i in range(count)
    ]
    for put in puts:
        put.start()
    for put in puts:
        put.wait()


def finish(*values):
    anywhere = pl.BlockSpec(memory_space=pl.ANY)
    return pl.pallas_call(
        finish_kernel,
        out_shape=tuple(pltpu.HBM(value.shape, value.dtype) for value in values),
        in_specs=[anywhere] * len(values),
        out_specs=(anywhere,) * len(values),
        scratch_shapes=[pltpu.SemaphoreType.DMA((len(values),))],
        compiler_params=pltpu.CompilerParams(vmem_limit_bytes=8 * 1024 * 1024),
        name="finish",
    )(*values)


def shards(query_act, rotated_keys, value_input, grad_out, out_weight, doc_lengths):
    dp_count, tensor_count = lax.axis_size("dp"), lax.axis_size("tensor")
    spots = dp_count // 2
    fars = tensor_count // 2 - 1
    seq_len = query_act.shape[1]
    depth, width = out_weight.shape
    half = width // 2
    heads = depth // HEAD_SIZE
    forward_rows, part_rows, back_rows, window = block_sizes(seq_len, tensor_count)
    parts = seq_len // 2 // part_rows
    pieces = seq_len // tensor_count // part_rows
    dma = pltpu.SemaphoreType.DMA
    anywhere = pl.BlockSpec(memory_space=pl.ANY)
    low, full = jnp.bfloat16, jnp.float32
    kv_shape = pltpu.VMEM((seq_len // 2, HEAD_SIZE), low)
    query_grad, key_grad, value_grad, weight_grad = pl.pallas_call(
        functools.partial(exchange_kernel, dp_count, tensor_count),
        out_shape=(
            pltpu.VMEM((seq_len, depth), low),
            kv_shape,
            kv_shape,
            pltpu.VMEM((depth, width), full),
        ),
        in_specs=[pl.BlockSpec(memory_space=pltpu.HBM)] * 6,
        out_specs=(anywhere,) * 4,
        scratch_shapes=[
            pltpu.VMEM((2, spots, seq_len, half), low),
            pltpu.VMEM((2, spots, 2 * depth, half), low),
            pltpu.VMEM((3, spots, depth, half), low),
            pltpu.VMEM((3, spots + 1, depth, half), low),
            pltpu.VMEM((spots, depth, half), low),
            pltpu.VMEM((spots, depth, half), low),
            pltpu.VMEM((seq_len, 2 * depth), full),
            pltpu.VMEM((seq_len, depth), low),
            pltpu.VMEM((seq_len, HEAD_SIZE), low),
            pltpu.VMEM((seq_len, HEAD_SIZE), low),
            pltpu.VMEM((seq_len, depth), low),
            pltpu.VMEM((2, depth, half), full),
            pltpu.VMEM((heads, seq_len, window), full),
            pltpu.VMEM((heads, seq_len // back_rows, window, back_rows), low),
            pltpu.VMEM((seq_len, depth), low),
            pltpu.VMEM((depth, seq_len), low),
            pltpu.VMEM((2, depth, seq_len), low),
            pltpu.VMEM((seq_len // 2, 2 * depth), low),
            pltpu.VMEM((seq_len // 2, 2 * depth), low),
            pltpu.VMEM((seq_len // 2, depth), low),
            pltpu.VMEM((2, seq_len // 2, depth), low),
            pltpu.VMEM((depth, half), low),
            pltpu.VMEM((depth, half), low),
            pltpu.VMEM((2, seq_len, HEAD_SIZE), full),
            pltpu.VMEM((2, seq_len // 2, HEAD_SIZE), full),
            pltpu.VMEM((2, seq_len // 2, HEAD_SIZE), low),
            pltpu.SMEM(doc_lengths.shape, jnp.int32),
            dma((3,)),
            dma,
            dma,
            dma((fars,)),
            dma((fars, spots + pieces)),
            dma((fars,)),
            dma((fars, spots + pieces)),
            dma((2,)),
            dma((3, spots)),
            dma((3, spots + 1)),
            dma,
            dma((spots + 1,)),
            dma,
            dma((spots,)),
            dma((3,)),
            dma((3,)),
            dma,
            dma((parts,)),
            dma,
            dma((parts,)),
            dma,
            dma,
            dma,
            dma,
            dma((4,)),
            dma,
            dma,
            dma((2,)),
        ],
        compiler_params=pltpu.CompilerParams(
            collective_id=0, has_side_effects=True, vmem_limit_bytes=56 * 1024 * 1024
        ),
        name="exchange",
    )(grad_out[0], out_weight, query_act[0], rotated_keys[0], value_input[0], doc_lengths)
    query_grad, key_grad, value_grad, weight_grad = finish(
        query_grad, key_grad, value_grad, weight_grad
    )
    return (query_grad[None], key_grad[None, None], value_grad[None, None], weight_grad)


def solution(mesh):
    placed = (
        P("dp", None, "tensor"),
        P("dp", None, None),
        P("dp", None, None),
        P("dp", "tensor", None),
        P("tensor", "dp"),
        P("dp", None),
    )
    return jax.shard_map(
        shards,
        mesh=mesh,
        in_specs=placed,
        out_specs=(
            P("dp", None, "tensor"),
            P("dp", "tensor", None, None),
            P("dp", "tensor", None, None),
            P("tensor", "dp"),
        ),
        check_vma=False,
    )
```

time: 89.1 us -> 86.6 us (0.972)
  the two profiles are of different devices: /device:TPU:0 before, /device:TPU:9 now
where the time goes in v5:
time: 86.6 us; the launch traced here: 86.4 us
  Pallas kernels  85.6 us (99%)
    pallas_call x1, Pallas kernels, shards(): pl.pallas_call(functools.partial(exchange_kernel, dp_count, tensor_count)...  84.4 us

profile of v5, /device:TPU:9, one launch (start us, length us, event | category | flops | bytes accessed | tf_op | source)
XLA Modules:
  0.0 86.4 jit_solution(18132692291987864582)
XLA Ops:
  0.6 84.4 %exchange.1 = (bf16[1024,256]{1,0:T(8,128)(2,1)S(1)}, bf16[512,128]{1,0:T(8,128)(2,1)S(1)}, bf16[512,128]{1,0:T(8,128)(2,1)S(1)}, f32[256,1024]{1,0:T(8,128)S(1)}) custom-call(bf16[256,8192]{1,0:T(8,128)(2,1)} %bitcast.7, bf16[256,1024]{1,0:T(8,128)(2,1)} %weight_ref.1, bf16[1024,256]{1,0:T(8,128)(2,1)} %bitcast.8, bf16[1024,256]{1,0:T(8,128)(2,1)} %bitcast.9, ...), custom_call_target="tpu_custom_call" | custom-call | tf_op jit(solution)/shard_map/exchange/pallas_call | solution.py:851
  85.0 1.3 %finish.1 = (bf16[1024,256]{1,0:T(8,128)(2,1)}, bf16[512,128]{1,0:T(8,128)(2,1)}, bf16[512,128]{1,0:T(8,128)(2,1)}, f32[256,1024]{1,0:T(8,128)}) custom-call(bf16[1024,256]{1,0:T(8,128)(2,1)S(1)} %get-tuple-element.12.refs_0_, bf16[512,128]{1,0:T(8,128)(2,1)S(1)} %get-tuple-element.13.refs_1_, bf16[512,128]{1,0:T(8,128)(2,1)S(1)} %get-tuple-element.14.refs_2_, ...), custom_call_target="tpu_custom_call" | custom-call | tf_op jit(solution)/shard_map/finish/pallas_call | solution.py:825

commit v6 on v5

--- a/solution.py
+++ b/solution.py
@@ -303,13 +303,13 @@
     def part_slice(part):
         return slice(part_start(part), part_start(part) + part_rows)
 
-    def share_copy(part):
+    def share_copy(part, slot):
         here = part_slice(part)
         return remote(
-            share_out.at[here],
-            share_in.at[here],
+            share_out.at[here, slots[slot]],
+            share_in.at[here, slots[slot]],
             share_send,
-            share_recv.at[part],
+            share_recv.at[part, slot],
             twin,
             tensor_index,
         )
@@ -594,20 +594,23 @@
         )
 
     def share(piece):
-        for part in range(len(parts)):
-            if parts[part][2] == piece:
-                here = part_slice(part)
-                there = slice(half_rows + here.start, half_rows + here.stop)
-                share_out[here] = accum[there].astype(jnp.bfloat16)
-                share_copy(part).start()
-
-    def settle(part):
+        for slot in (1, 0):
+            for part in range(len(parts)):
+                if parts[part][2] == piece:
+                    here = part_slice(part)
+                    there = slice(half_rows + here.start, half_rows + here.stop)
+                    share_out[here, slots[slot]] = accum[there, slots[slot]].astype(jnp.bfloat16)
+                    share_copy(part, slot).start()
+
+    def settle(part, slot):
         here = part_slice(part)
-        share_copy(part).wait_recv()
-        both = (accum[here] + share_in[here].astype(jnp.float32)).astype(jnp.bfloat16)
-        turn_out[here] = both[:, slots[1]]
-        turn_copy(part).start()
-        out_grad[0, here] = both[:, slots[0]]
+        share_copy(part, slot).wait_recv()
+        both = accum[here, slots[slot]] + share_in[here, slots[slot]].astype(jnp.float32)
+        if slot:
+            turn_out[here] = both.astype(jnp.bfloat16)
+            turn_copy(part).start()
+        else:
+            out_grad[0, here] = both.astype(jnp.bfloat16)
 
     def finished(part):
         start = part_start(part)
@@ -655,14 +658,6 @@
     drain(weights.at[:, spot, slots[0]], own_sem.at[1])
     drain(outs_t.at[0, :, slice(0, half_rows)], own_sem.at[2])
     drain(grads.at[:, :, local_rows(0, pair, 1 - core)], near_recv)
-    def pass_rest(far):
-        def work(way, owner):
-            @pl.when(owner != first_block)
-            def _():
-                far_pass(owner)
-
-        owner_do(far, work)
-
     drain(outs_t.at[1, :, slice(0, half_rows)], outs_recv.at[0])
     for which_pair in range(pairs):
         outs_copy(3, which_pair).start()
@@ -687,13 +682,21 @@
     for piece in range(pieces):
         for route in range(fars):
             last_copy(route, piece).start()
-    def rest_do(far, work):
-        def inner(way, owner):
+    def stage(far, way, where):
+        owner = spot + way * far
+
+        @pl.when(reaches(way, far))
+        def _():
             @pl.when(owner != first_block)
             def _():
-                work(owner)
-
-        owner_do(far, inner)
+                @pl.when(where)
+                def _():
+                    far_pass(owner)
+                    pass_wait(owner)
+                    cross(owner)
+
+    inside = spot % (spots - 1) != 0
+    early = spots == 4
 
     def both_project(far):
         owner_do(far, lambda way, owner: project(owner, 1))
@@ -717,13 +720,17 @@
     hop_project(1)
     for far in range(spots - 2, 0, -1):
         hop = spots - far + 1
-        pass_rest(far)
-        rest_do(far, pass_wait)
-        rest_do(far, cross)
+        for way in ways:
+            if early and far == 1 and way > 0:
+                stage(far, way, spot % (spots - 1) == 0)
+            else:
+                stage(far, way, spot >= 0)
         total_step(far, 1)
         total_step(far, 0)
         if far == spots - 2:
             total_first(2, False)
+            if early:
+                stage(1, 1, inside)
             hop_project(2)
         if far <= spots // 2:
             both_project(far)
@@ -753,29 +760,66 @@
         if piece + 1 < pieces:
             last_pass(piece + 1)
 
-    total_step(1, 2)
-    back_out[...] = total_final(1).astype(jnp.bfloat16)
-    later = []
-    for part in range(len(parts)):
-        settle(part)
-        back_copy(part).start()
+    def turned(part):
+        turn_copy(part).wait_recv()
+        if finished(part) is not None:
+            backward(1, finished(part))
+
+    def settled(part):
+        settle(part, 0)
         if finished(part) is not None:
             backward(0, finished(part))
-        if part == len(parts) - 2:
-            weight_grad_ref[0] = total_final(0)
-        for earlier in later:
-            turn_copy(earlier).wait_recv()
-            if finished(earlier) is not None:
-                backward(1, finished(earlier))
-        later = [part]
+
+    def back_start(piece):
+        for part in range(len(parts)):
+            if parts[part][2] == piece:
+                back_copy(part).start()
+
+    groups = [
+        [part for part in range(len(parts)) if parts[part][2] == piece] for piece in range(pieces)
+    ]
+    for piece, group in enumerate(groups):
+        before = groups[piece - 1] if piece else []
+        for number, part in enumerate(group):
+            settle(part, 1)
+            if piece == 0 and number == 0:
+                total_step(1, 2)
+            if number < len(before):
+                turned(before[number])
+        for part in before[len(group) :]:
+            turned(part)
+        if piece == 0:
+            back_out[...] = total_final(1).astype(jnp.bfloat16)
+        back_start(piece)
+        for part in group:
+            settled(part)
+    for part in groups[-1]:
+        turned(part)
+    kv_copy.start()
     weight_grad_ref[1] = total_final(2)
     weight_put(1).start()
-    turn_copy(later[0]).wait_recv()
-    backward(1, finished(later[0]))
-    kv_copy.start()
+    part = total_final(0)
     drain(back_in, back_recv)
-    weight_grad_ref[0] = weight_grad_ref[0] + back_in[...].astype(jnp.float32)
+    weight_grad_ref[0] = part + back_in[...].astype(jnp.float32)
     weight_put(0).start()
+    drain(grads.at[:, :, local_rows(0, pair, core)], near_send)
+    for route in range(fars):
+        drain(grads.at[:, :, local_rows(0, pair, core)], far_send.at[route])
+        drain(grads.at[:, :, local_rows(0, pair, core)], pass_send.at[route])
+    for index in range(3):
+        drain(outs_t.at[0, :, slice(0, half_rows)], outs_send.at[index])
+    drain(share_out, share_send)
+    drain(turn_out, turn_send)
+    drain(query_grad_ref, query_sem)
+    drain(sums_in.at[0], wing_send)
+    drain(cross_out, cross_send)
+    drain(back_out, back_send)
+    for way in ways:
+
+        @pl.when(exists(way))
+        def _():
+            drain(grads.at[0, :, slice(0, 3 * depth)], line_send.at[(1 - way) // 2])
+
     mine = pl.ds(pl.multiple_of(core * half_rows, half_rows), half_rows)
     kv_copy.wait()
     kv_done[...] = (kv_grads[:, mine] + kv_in[...]).astype(jnp.bfloat16)
@@ -785,28 +829,9 @@
     ]
     for put in kv_puts:
         put.start()
-
-    drain(grads.at[:, :, local_rows(0, pair, core)], near_send)
-    for route in range(fars):
-        drain(grads.at[:, :, local_rows(0, pair, core)], far_send.at[route])
-        drain(grads.at[:, :, local_rows(0, pair, core)], pass_send.at[route])
-    for index in range(3):
-        drain(outs_t.at[0, :, slice(0, half_rows)], outs_send.at[index])
-    drain(share_out, share_send)
-    drain(turn_out, turn_send)
-    drain(query_grad_ref, query_sem)
+    drain(weight_grad_ref, put_sem)
     for put in kv_puts:
         put.wait()
-    drain(sums_in.at[0], wing_send)
-    drain(cross_out, cross_send)
-    drain(back_out, back_send)
-    for way in ways:
-
-        @pl.when(exists(way))
-        def _():
-            drain(grads.at[0, :, slice(0, 3 * depth)], line_send.at[(1 - way) // 2])
-
-    drain(weight_grad_ref, put_sem)
 
 
 def finish_kernel(*refs):
@@ -903,7 +928,7 @@
             dma((3,)),
             dma((3,)),
             dma,
-            dma((parts,)),
+            dma((parts, 2)),
             dma,
             dma((parts,)),
             dma,

time: 86.6 us -> 81.9 us (0.946)
  the two profiles are of different devices: /device:TPU:9 before, /device:TPU:0 now
where the time goes in v6:
time: 81.9 us; the launch traced here: 81.6 us
  Pallas kernels  80.7 us (99%)
  between operations  0.82 us (1%)
    pallas_call x1, Pallas kernels, shards(): pl.pallas_call(functools.partial(exchange_kernel, dp_count, tensor_count)...  79.5 us

profile of v6, /device:TPU:0, one launch (start us, length us, event | category | flops | bytes accessed | tf_op | source)
XLA Modules:
  0.0 81.6 jit_solution(14934972544428196855)
XLA Ops:
  0.6 79.5 %exchange.1 = (bf16[1024,256]{1,0:T(8,128)(2,1)S(1)}, bf16[512,128]{1,0:T(8,128)(2,1)S(1)}, bf16[512,128]{1,0:T(8,128)(2,1)S(1)}, f32[256,1024]{1,0:T(8,128)S(1)}) custom-call(bf16[256,8192]{1,0:T(8,128)(2,1)} %bitcast.7, bf16[256,1024]{1,0:T(8,128)(2,1)} %weight_ref.1, bf16[1024,256]{1,0:T(8,128)(2,1)} %bitcast.8, bf16[1024,256]{1,0:T(8,128)(2,1)} %bitcast.9, ...), custom_call_target="tpu_custom_call" | custom-call | tf_op jit(solution)/shard_map/exchange/pallas_call | solution.py:876
  80.1 1.3 %finish.1 = (bf16[1024,256]{1,0:T(8,128)(2,1)}, bf16[512,128]{1,0:T(8,128)(2,1)}, bf16[512,128]{1,0:T(8,128)(2,1)}, f32[256,1024]{1,0:T(8,128)}) custom-call(bf16[1024,256]{1,0:T(8,128)(2,1)S(1)} %get-tuple-element.12.refs_0_, bf16[512,128]{1,0:T(8,128)(2,1)S(1)} %get-tuple-element.13.refs_1_, bf16[512,128]{1,0:T(8,128)(2,1)S(1)} %get-tuple-element.14.refs_2_, ...), custom_call_target="tpu_custom_call" | custom-call | tf_op jit(solution)/shard_map/finish/pallas_call | solution.py:850

commit v7 on v6

--- a/solution.py
+++ b/solution.py
@@ -18,7 +18,7 @@
     forward_rows = min(256, seq_len)
     part_rows = rows // max(1, rows // 128)
     block_rows = max(part_rows, min(128, 2 * rows))
-    return forward_rows, part_rows, block_rows, seq_len // 2 + forward_rows
+    return forward_rows, part_rows, block_rows, seq_len // 2 + forward_rows, seq_len // 2 + block_rows
 
 
 def exchange_kernel(
@@ -108,7 +108,7 @@
     heads = depth // HEAD_SIZE
     half_rows = seq_len // 2
     score_scale = HEAD_SIZE ** (-0.5)
-    forward_rows, part_rows, back_rows, window = block_sizes(seq_len, tensor_count)
+    forward_rows, part_rows, back_rows, window, narrow = block_sizes(seq_len, tensor_count)
     kv_columns = pl.ds(pl.multiple_of(tensor_index // 2 * HEAD_SIZE, HEAD_SIZE), HEAD_SIZE)
     slots = (slice(0, depth), slice(depth, 2 * depth))
     sides = (slice(0, half), slice(half, width))
@@ -387,18 +387,18 @@
     def dot(left, right, dims):
         return lax.dot_general(left, right, dims, preferred_element_type=jnp.float32)
 
-    def window_start(index):
-        skip, total = half_rows // forward_rows, seq_len // forward_rows
-        past = (index + total - skip) // total
-        return past * (index - skip) * forward_rows
+    def first_key(block, block_rows):
+        skip, total = half_rows // block_rows, seq_len // block_rows
+        past = (block + total - skip) // total
+        return past * (block - skip) * block_rows
 
     def window_keys(index):
-        return pl.ds(pl.multiple_of(window_start(index), forward_rows), window)
+        return pl.ds(first_key(index, forward_rows), window)
 
     def forward(index):
         here = pl.ds(pl.multiple_of(index * forward_rows, forward_rows), forward_rows)
         query_places = index * forward_rows + lax.broadcasted_iota(jnp.int32, (forward_rows, 1), 0)
-        key_places = window_start(index) + lax.broadcasted_iota(
+        key_places = first_key(index, forward_rows) + lax.broadcasted_iota(
             jnp.int32, (forward_rows, window), 1
         )
         doc_start = jnp.zeros((forward_rows, 1), jnp.int32)
@@ -415,13 +415,14 @@
             row_max = jnp.max(scores, axis=1, keepdims=True)
             total = jnp.sum(jnp.exp(scores - row_max), axis=1, keepdims=True)
             prob = jnp.exp(scores - (row_max + jnp.log(total)))
-            probs[head, here] = prob
             out = jnp.dot(prob.astype(jnp.bfloat16), values, preferred_element_type=jnp.float32)
             outs[here, lanes] = out.astype(jnp.bfloat16)
             outs_own[lanes, here] = out.T.astype(jnp.bfloat16)
             for part in range(forward_rows // back_rows):
-                piece = prob[part * back_rows : (part + 1) * back_rows]
                 block = index * (forward_rows // back_rows) + part
+                skip = first_key(block, back_rows) - first_key(index, forward_rows)
+                piece = prob[part * back_rows : (part + 1) * back_rows, skip : skip + narrow]
+                probs[head, block * back_rows : (block + 1) * back_rows] = piece
                 probs_t[head, block] = piece.T.astype(jnp.bfloat16)
 
     def backward(which, start):
@@ -429,24 +430,38 @@
         place = start // (2 * rows) * 4 * rows + start % (2 * rows)
         block = place // back_rows + whose * (2 * rows // back_rows)
         here = pl.ds(pl.multiple_of(block * back_rows, back_rows), back_rows)
-        seen = window_keys(block // (forward_rows // back_rows))
+        seen = pl.ds(pl.multiple_of(first_key(block, back_rows), back_rows), narrow)
         keys, values = key_ref[seen], value_ref[seen]
-        key_total, value_total = kv_grads[0, seen], kv_grads[1, seen]
+        grads_low, products, deltas, dscores = [], [], [], []
         for head in range(heads):
             lanes = slice(head * HEAD_SIZE, (head + 1) * HEAD_SIZE)
             grad = out_grad[which, start : start + back_rows, lanes]
-            delta = jnp.sum(
-                grad.astype(jnp.float32) * outs[here, lanes].astype(jnp.float32), axis=1, keepdims=True
+            grads_low.append(grad)
+            products.append(dot(grad, values, nt))
+            deltas.append(
+                jnp.sum(
+                    grad.astype(jnp.float32) * outs[here, lanes].astype(jnp.float32),
+                    axis=1,
+                    keepdims=True,
+                )
             )
-            dscore = probs[head, here] * (dot(grad, values, nt) - delta) * score_scale
-            dscore = dscore.astype(jnp.bfloat16)
+        value_total = kv_grads[1, seen]
+        for head in range(heads):
+            value_total += jnp.dot(
+                probs_t[head, block], grads_low[head], preferred_element_type=jnp.float32
+            )
+        kv_grads[1, seen] = value_total
+        for head in range(heads):
+            dscore = probs[head, here] * (products[head] - deltas[head]) * score_scale
+            dscores.append(dscore.astype(jnp.bfloat16))
+        key_total = kv_grads[0, seen]
+        for head in range(heads):
+            lanes = slice(head * HEAD_SIZE, (head + 1) * HEAD_SIZE)
+            key_total += dot(dscores[head], query_ref[here, lanes], tn)
             query_grad_ref[here, lanes] = jnp.dot(
-                dscore, keys, preferred_element_type=jnp.float32
+                dscores[head], keys, preferred_element_type=jnp.float32
             ).astype(jnp.bfloat16)
-            key_total += dot(dscore, query_ref[here, lanes], tn)
-            value_total += jnp.dot(probs_t[head, block], grad, preferred_element_type=jnp.float32)
         kv_grads[0, seen] = key_total
-        kv_grads[1, seen] = value_total
         pltpu.make_async_copy(
             query_grad_ref.at[here], query_grad_out.at[here], query_sem
         ).start()
@@ -573,10 +588,8 @@
                 tensor_index,
             ).start()
 
-    def total_final(chunk):
-        side, slot = chunks[chunk]
-        part = sum_part(slot, side, spot)
-        if side:
+    def total_final(chunk, part):
+        if chunks[chunk][0]:
             drain(cross_in.at[spot], cross_recv.at[spot])
             part = part + cross_in[spot].astype(jnp.float32)
         for way, index in ((-1, spot), (1, spots)):
@@ -789,19 +802,19 @@
         for part in before[len(group) :]:
             turned(part)
         if piece == 0:
-            back_out[...] = total_final(1).astype(jnp.bfloat16)
+            back_out[...] = total_final(1, sum_part(1, 0, spot)).astype(jnp.bfloat16)
         back_start(piece)
-        for part in group:
+        for number, part in enumerate(group):
             settled(part)
+            if piece == 0 and number < 2:
+                weight_grad_ref[number] = sum_part(0, number, spot)
+            if piece == pieces - 1 and number == len(group) - 2:
+                weight_grad_ref[0] = total_final(0, weight_grad_ref[0])
     for part in groups[-1]:
         turned(part)
     kv_copy.start()
-    weight_grad_ref[1] = total_final(2)
+    weight_grad_ref[1] = total_final(2, weight_grad_ref[1])
     weight_put(1).start()
-    part = total_final(0)
-    drain(back_in, back_recv)
-    weight_grad_ref[0] = part + back_in[...].astype(jnp.float32)
-    weight_put(0).start()
     drain(grads.at[:, :, local_rows(0, pair, core)], near_send)
     for route in range(fars):
         drain(grads.at[:, :, local_rows(0, pair, core)], far_send.at[route])
@@ -820,15 +833,17 @@
         def _():
             drain(grads.at[0, :, slice(0, 3 * depth)], line_send.at[(1 - way) // 2])
 
+    drain(back_in, back_recv)
+    weight_grad_ref[0] = weight_grad_ref[0] + back_in[...].astype(jnp.float32)
+    weight_put(0).start()
     mine = pl.ds(pl.multiple_of(core * half_rows, half_rows), half_rows)
-    kv_copy.wait()
-    kv_done[...] = (kv_grads[:, mine] + kv_in[...]).astype(jnp.bfloat16)
-    kv_puts = [
-        pltpu.make_async_copy(kv_done.at[which], to, kv_sem.at[which])
-        for which, to in enumerate((key_grad_out, value_grad_out))
-    ]
-    for put in kv_puts:
-        put.start()
+    kv_copy.wait_recv()
+    kv_puts = []
+    for which, to in enumerate((key_grad_out, value_grad_out)):
+        kv_done[which] = (kv_grads[which, mine] + kv_in[which]).astype(jnp.bfloat16)
+        kv_puts.append(pltpu.make_async_copy(kv_done.at[which], to, kv_sem.at[which]))
+        kv_puts[which].start()
+    kv_copy.wait_send()
     drain(weight_grad_ref, put_sem)
     for put in kv_puts:
         put.wait()
@@ -866,7 +881,7 @@
     depth, width = out_weight.shape
     half = width // 2
     heads = depth // HEAD_SIZE
-    forward_rows, part_rows, back_rows, window = block_sizes(seq_len, tensor_count)
+    forward_rows, part_rows, back_rows, window, narrow = block_sizes(seq_len, tensor_count)
     parts = seq_len // 2 // part_rows
     pieces = seq_len // tensor_count // part_rows
     dma = pltpu.SemaphoreType.DMA
@@ -896,8 +911,8 @@
             pltpu.VMEM((seq_len, HEAD_SIZE), low),
             pltpu.VMEM((seq_len, depth), low),
             pltpu.VMEM((2, depth, half), full),
-            pltpu.VMEM((heads, seq_len, window), full),
-            pltpu.VMEM((heads, seq_len // back_rows, window, back_rows), low),
+            pltpu.VMEM((heads, seq_len, narrow), full),
+            pltpu.VMEM((heads, seq_len // back_rows, narrow, back_rows), low),
             pltpu.VMEM((seq_len, depth), low),
             pltpu.VMEM((depth, seq_len), low),
             pltpu.VMEM((2, depth, seq_len), low),

time: 81.9 us -> 81.7 us (level)
  no operation moved by 1% of the time
where the time goes in v7:
time: 81.7 us; the launch traced here: 81.5 us
  Pallas kernels  80.7 us (99%)
    pallas_call x1, Pallas kernels, shards(): pl.pallas_call(functools.partial(exchange_kernel, dp_count, tensor_count)...  79.5 us

profile of v7, /device:TPU:0, one launch (start us, length us, event | category | flops | bytes accessed | tf_op | source)
XLA Modules:
  0.0 81.5 jit_solution(4960181573809843617)
XLA Ops:
  0.6 79.5 %exchange.1 = (bf16[1024,256]{1,0:T(8,128)(2,1)S(1)}, bf16[512,128]{1,0:T(8,128)(2,1)S(1)}, bf16[512,128]{1,0:T(8,128)(2,1)S(1)}, f32[256,1024]{1,0:T(8,128)S(1)}) custom-call(bf16[256,8192]{1,0:T(8,128)(2,1)} %bitcast.7, bf16[256,1024]{1,0:T(8,128)(2,1)} %weight_ref.1, bf16[1024,256]{1,0:T(8,128)(2,1)} %bitcast.8, bf16[1024,256]{1,0:T(8,128)(2,1)} %bitcast.9, ...), custom_call_target="tpu_custom_call" | custom-call | tf_op jit(solution)/shard_map/exchange/pallas_call | solution.py:891
  80.1 1.3 %finish.1 = (bf16[1024,256]{1,0:T(8,128)(2,1)}, bf16[512,128]{1,0:T(8,128)(2,1)}, bf16[512,128]{1,0:T(8,128)(2,1)}, f32[256,1024]{1,0:T(8,128)}) custom-call(bf16[1024,256]{1,0:T(8,128)(2,1)S(1)} %get-tuple-element.12.refs_0_, bf16[512,128]{1,0:T(8,128)(2,1)S(1)} %get-tuple-element.13.refs_1_, bf16[512,128]{1,0:T(8,128)(2,1)S(1)} %get-tuple-element.14.refs_2_, ...), custom_call_target="tpu_custom_call" | custom-call | tf_op jit(solution)/shard_map/finish/pallas_call | solution.py:865

commit v8 on v7

--- a/solution.py
+++ b/solution.py
@@ -833,9 +833,6 @@
         def _():
             drain(grads.at[0, :, slice(0, 3 * depth)], line_send.at[(1 - way) // 2])
 
-    drain(back_in, back_recv)
-    weight_grad_ref[0] = weight_grad_ref[0] + back_in[...].astype(jnp.float32)
-    weight_put(0).start()
     mine = pl.ds(pl.multiple_of(core * half_rows, half_rows), half_rows)
     kv_copy.wait_recv()
     kv_puts = []
@@ -843,6 +840,9 @@
         kv_done[which] = (kv_grads[which, mine] + kv_in[which]).astype(jnp.bfloat16)
         kv_puts.append(pltpu.make_async_copy(kv_done.at[which], to, kv_sem.at[which]))
         kv_puts[which].start()
+    drain(back_in, back_recv)
+    weight_grad_ref[0] = weight_grad_ref[0] + back_in[...].astype(jnp.float32)
+    weight_put(0).start()
     kv_copy.wait_send()
     drain(weight_grad_ref, put_sem)
     for put in kv_puts:

time: 81.7 us -> 81.3 us (level)
  no operation moved by 1% of the time
where the time goes in v8:
time: 81.3 us; the launch traced here: 81.1 us
  Pallas kernels  80.3 us (99%)
    pallas_call x1, Pallas kernels, shards(): pl.pallas_call(functools.partial(exchange_kernel, dp_count, tensor_count)...  79 us

profile of v8, /device:TPU:0, one launch (start us, length us, event | category | flops | bytes accessed | tf_op | source)
XLA Modules:
  0.0 81.1 jit_solution(8485013256945025677)
XLA Ops:
  0.6 79.0 %exchange.1 = (bf16[1024,256]{1,0:T(8,128)(2,1)S(1)}, bf16[512,128]{1,0:T(8,128)(2,1)S(1)}, bf16[512,128]{1,0:T(8,128)(2,1)S(1)}, f32[256,1024]{1,0:T(8,128)S(1)}) custom-call(bf16[256,8192]{1,0:T(8,128)(2,1)} %bitcast.7, bf16[256,1024]{1,0:T(8,128)(2,1)} %weight_ref.1, bf16[1024,256]{1,0:T(8,128)(2,1)} %bitcast.8, bf16[1024,256]{1,0:T(8,128)(2,1)} %bitcast.9, ...), custom_call_target="tpu_custom_call" | custom-call | tf_op jit(solution)/shard_map/exchange/pallas_call | solution.py:891
  79.6 1.3 %finish.1 = (bf16[1024,256]{1,0:T(8,128)(2,1)}, bf16[512,128]{1,0:T(8,128)(2,1)}, bf16[512,128]{1,0:T(8,128)(2,1)}, f32[256,1024]{1,0:T(8,128)}) custom-call(bf16[1024,256]{1,0:T(8,128)(2,1)S(1)} %get-tuple-element.12.refs_0_, bf16[512,128]{1,0:T(8,128)(2,1)S(1)} %get-tuple-element.13.refs_1_, bf16[512,128]{1,0:T(8,128)(2,1)S(1)} %get-tuple-element.14.refs_2_, ...), custom_call_target="tpu_custom_call" | custom-call | tf_op jit(solution)/shard_map/finish/pallas_call | solution.py:865
